TPU v7x, 32 devices: a whole 2x2x4 slice. The times are simulated.
32 devices in a mesh: dp: 16 (over z, y, x), tensor: 2 (over core).
Axes of the slice: x: 2, y: 2, z: 4, core: 2. Of those that a mesh axis runs over, the one named last changes fastest.
Arguments:
- pool: bfloat16 [4096, 2048], P('dp', 'tensor'), may hold values from -6 to 6
- select: int32 [2048], P('dp'), may hold values from 0 to 4095, as said below
- reward_w: bfloat16 [2048], P('tensor'), may hold values from -0.125 to 0.125
- routes: int32 [2048, 6], P('dp'), may hold values from 0 to 15, all different within a row; in each aligned block of 128 rows (0 to 127, 128 to 255, ...) at most 60 rows name the same one
- gates: float32 [2048, 6], P('dp'), may hold values from 0.05 to 0.5
- target: bfloat16 [2048, 2048], P('dp', 'tensor'), may hold values from -6 to 6
- w_gate: bfloat16 [16, 1408, 2048], P('dp', 'tensor'), may hold values from -0.125 to 0.125
- w_up: bfloat16 [16, 1408, 2048], P('dp', 'tensor'), may hold values from -0.125 to 0.125
- w_down: bfloat16 [16, 1408, 2048], P('dp', 'tensor'), may hold values from -0.15625 to 0.15625
Outputs:
- mixed: bfloat16 [2048, 2048], P('dp', 'tensor')
- grad_gate: bfloat16 [16, 1408, 2048], P('dp', 'tensor')
- grad_up: bfloat16 [16, 1408, 2048], P('dp', 'tensor')
- grad_down: bfloat16 [16, 1408, 2048], P('dp', 'tensor')
Inputs may be any that keep to these rules, and one draw needn't show every extreme that they name: The 128 entries of aligned block i of select are distinct rows of pool's block i, rows i * 256 to (i + 1) * 256 - 1. `routes`: each row names 6 different experts. In the 128 rows of one device no expert is named more than 60 times, a bound that some block reaches.
All inputs are finite; a program needn't handle non-finite values.
Results may differ from a plain program's by a relative error of at most 0.015.
Values may be sent and summed in bfloat16 or wider, within the bound.
A program may use at most 128 MiB of HBM per device.

v0:
```python
import jax
import jax.numpy as jnp
from jax import lax
from jax.sharding import PartitionSpec as P


def slot_factor(route_hit, weights):
    return jnp.sum(jnp.where(route_hit, weights.reshape(-1)[:, None], 0.0), axis=0)


def local(pool, select, reward_w, routes, gates, target, w_gate, w_up, w_down):
    pool_rows = pool.shape[0]
    local_rows = select - lax.axis_index("dp") * pool_rows
    chosen = jnp.take(pool, local_rows, axis=0)
    sel_rows, top_count = routes.shape
    owners = lax.axis_size("dp")
    exp_dev = w_gate.shape[0]
    experts = owners * exp_dev
    capacity = 5 * sel_rows * top_count // (4 * experts)
    slot_count = experts * capacity
    flat_routes = routes.reshape(-1)
    onehot = (flat_routes[:, None] == jnp.arange(experts, dtype=jnp.int32)[None, :]).astype(
        jnp.int32
    )
    before = jnp.cumsum(onehot, axis=0) - onehot
    slot_rank = jnp.sum(before * onehot, axis=1)
    slot_place = flat_routes * capacity + slot_rank
    route_hit = slot_place[:, None] == jnp.arange(slot_count, dtype=jnp.int32)[None, :]
    route_pick = route_hit.astype(jnp.bfloat16).reshape(sel_rows, top_count, slot_count)
    token_pick = jnp.sum(route_pick, axis=1)
    reward = lax.psum(jnp.dot(chosen, reward_w, preferred_element_type=jnp.float32), "tensor")
    keep_scale = jax.nn.sigmoid(reward)
    slot_scale = slot_factor(route_hit, keep_scale[:, None] * gates)
    token_send = jnp.einsum(
        "sp,sd->pd", token_pick, chosen, preferred_element_type=jnp.float32
    ).astype(jnp.bfloat16)
    picked_target = jnp.einsum("sp,sd->pd", token_pick, target, preferred_element_type=jnp.float32)
    cot_send = (picked_target * slot_scale[:, None]).astype(jnp.bfloat16)
    token_part, cot_part = (
        lax.all_to_all(token_send, "dp", split_axis=0, concat_axis=0, tiled=True),
        lax.all_to_all(cot_send, "dp", split_axis=0, concat_axis=0, tiled=True),
    )
    received_tokens, received_cots = (
        lax.all_gather(token_part, "tensor", axis=1, tiled=True),
        lax.all_gather(cot_part, "tensor", axis=1, tiled=True),
    )
    width = received_tokens.shape[1]
    token_rows = received_tokens.reshape(owners, exp_dev, capacity, width)
    cot_rows = received_cots.reshape(owners, exp_dev, capacity, width)
    gate_act = jnp.einsum("secd,efd->secf", token_rows, w_gate, preferred_element_type=jnp.float32)
    up_act = jnp.einsum("secd,efd->secf", token_rows, w_up, preferred_element_type=jnp.float32)
    sigmoid_gate = jax.nn.sigmoid(gate_act)
    hidden = (gate_act * sigmoid_gate * up_act).astype(jnp.bfloat16)
    partial_value = jnp.einsum("secf,efd->secd", hidden, w_down, preferred_element_type=jnp.float32)
    summed = lax.psum_scatter(
        partial_value.astype(jnp.bfloat16), "tensor", scatter_dimension=3, tiled=True
    )
    returned = lax.all_to_all(summed, "dp", split_axis=0, concat_axis=0, tiled=True).reshape(
        slot_count, -1
    )
    route_rows = jnp.einsum("skp,pd->skd", route_pick, returned, preferred_element_type=jnp.float32)
    mixed = jnp.sum(route_rows * gates[:, :, None], axis=1).astype(jnp.bfloat16)
    hidden_grad = jnp.einsum("secd,efd->secf", cot_rows, w_down, preferred_element_type=jnp.float32)
    gate_grad = (
        hidden_grad * up_act * sigmoid_gate * (1.0 + gate_act * (1.0 - sigmoid_gate))
    ).astype(jnp.bfloat16)
    up_grad = (hidden_grad * gate_act * sigmoid_gate).astype(jnp.bfloat16)
    grad_down = jnp.einsum(
        "secf,secd->efd", hidden, cot_rows, preferred_element_type=jnp.float32
    ).astype(jnp.bfloat16)
    grad_gate = jnp.einsum(
        "secf,secd->efd", gate_grad, token_rows, preferred_element_type=jnp.float32
    ).astype(jnp.bfloat16)
    grad_up = jnp.einsum(
        "secf,secd->efd", up_grad, token_rows, preferred_element_type=jnp.float32
    ).astype(jnp.bfloat16)
    return (mixed, grad_gate, grad_up, grad_down)


def solution(mesh):
    in_specs = (
        P("dp", "tensor"),
        P("dp"),
        P("tensor"),
        P("dp", None),
        P("dp", None),
        P("dp", "tensor"),
        P("dp", "tensor", None),
        P("dp", "tensor", None),
        P("dp", "tensor", None),
    )
    out_specs = (
        P("dp", "tensor"),
        P("dp", "tensor", None),
        P("dp", "tensor", None),
        P("dp", "tensor", None),
    )
    return jax.shard_map(local, mesh=mesh, in_specs=in_specs, out_specs=out_specs, check_vma=False)
```

profile of v0, /device:TPU:0, one launch (start us, length us, event | category | flops | bytes accessed | tf_op | source)
XLA Modules:
  0.0 241.6 jit_solution(12647398022362525615)
XLA Ops:
  7.2 0.9 copy.38
  8.1 0.1 eq.71
  8.3 0.1 eq.67
  8.4 1.7 reduce-window.6
  10.1 0.3 slice_reduce_fusion
  10.4 0.1 fusion.36
  10.5 0.1 reduce_sum.42
  10.7 0.1 copy.41
  10.7 0.7 multiply_add_fusion.1
  11.4 0.3 fusion.30
  11.8 0.7 compare_and_fusion
  12.5 2.2 gather_fusion
  14.6 2.0 convolution_convert_fusion
  16.6 3.6 %all_to_all.19 = bf16[16,60,1024]{2,1,0:T(8,128)(2,1)} reshape(bf16[960,1024]{1,0:T(8,128)(2,1)} %convolution_convert_fusion) | data formatting | bytes 3932160 | tf_op jit(solution)/shard_map/all_to_all | solution.py:40
  20.2 8.5 %all-to-all-start = ((bf16[16,60,1024]{2,1,0:T(8,128)(2,1)}), bf16[16,60,1024]{2,1,0:T(8,128)(2,1)}, u32[]{:S(2)}, u32[]{:S(2)}) async-start(bf16[16,60,1024]{2,1,0:T(8,128)(2,1)} %all_to_all.19), calls=%async_computation | async-start | bytes 4194304 | tf_op jit(solution)/shard_map/all_to_all | solution.py:40
  28.7 0.0 all-gather.3.cloned.1.call-start
  28.8 0.2 convolution_bitcast_fusion
  29.0 2.6 %psum.7 = f32[128]{0:T(128)S(1)} all-reduce(f32[128]{0:T(128)S(1)} %convolution_bitcast_fusion), channel_id=1, replica_groups=mesh['dp'=16,'tensor'=2] {'tensor'}, use_global_device_ids=true, to_apply=%region_6.7 | all-reduce | flops 128 | bytes 1024 | tf_op jit(solution)/shard_map/psum | solution.py:31
  31.7 0.1 copy.43
  31.8 0.1 broadcast_in_dim.35
  31.9 0.4 select_reduce_fusion
  32.3 39.5 %all-to-all-done = bf16[16,60,1024]{2,1,0:T(8,128)(2,1)} async-done(((bf16[16,60,1024]{2,1,0:T(8,128)(2,1)}), bf16[16,60,1024]{2,1,0:T(8,128)(2,1)}, u32[]{:S(2)}, u32[]{:S(2)}) %all-to-all-start) | async-done | bytes 1966112 | tf_op jit(solution)/shard_map/all_to_all | solution.py:40
  71.8 3.6 %all_to_all.21 = bf16[960,1024]{1,0:T(8,128)(2,1)} reshape(bf16[16,60,1024]{2,1,0:T(8,128)(2,1)} %all-to-all-done) | data formatting | bytes 3932160 | tf_op jit(solution)/shard_map/all_to_all | solution.py:40
  75.4 0.0 all-gather.3.cloned.1.call-update
  75.5 0.0 all-gather.5.cloned.1.call-start
  75.5 1.9 multiply_convert_fusion
  77.5 3.6 %all_to_all.23 = bf16[16,60,1024]{2,1,0:T(8,128)(2,1)} reshape(bf16[960,1024]{1,0:T(8,128)(2,1)} %multiply_convert_fusion) | data formatting | bytes 3932160 | tf_op jit(solution)/shard_map/all_to_all | solution.py:41
  81.0 58.3 %all_to_all.29 = bf16[16,60,1024]{2,1,0:T(8,128)(2,1)} all-to-all(bf16[16,60,1024]{2,1,0:T(8,128)(2,1)} %all_to_all.23), channel_id=1, replica_groups=mesh['dp'=16,'tensor'=2] {'dp'}, dimensions={0} | all-to-all | bytes 3932160 | tf_op jit(solution)/shard_map/all_to_all | solution.py:41
  139.3 3.6 %all_to_all.25 = bf16[960,1024]{1,0:T(8,128)(2,1)} reshape(bf16[16,60,1024]{2,1,0:T(8,128)(2,1)} %all_to_all.29) | data formatting | bytes 3932160 | tf_op jit(solution)/shard_map/all_to_all | solution.py:41
  142.9 0.0 all-gather.5.cloned.1.call-update
  142.9 0.2 reduce-scatter.2.cloned.1.call-start
  143.2 0.0 all-gather.3.cloned.1.call-done
  143.2 4.9 %reshape.132 = bf16[16,60,2048]{2,1,0:T(8,128)(2,1)} reshape(bf16[960,2048]{1,0:T(8,128)(2,1)} %all-gather.3.cloned.1.call-done) | data formatting | bytes 7864320 | tf_op jit(solution)/shard_map/reshape.10
  148.1 7.1 %fusion.22 = f32[16,60,704]{2,1,0:T(8,128)S(1)} fusion(bf16[16,60,2048]{2,1,0:T(8,128)(2,1)} %reshape.132, bf16[1,704,2048]{2,1,0:T(8,128)(2,1)} %param.15), kind=kOutput, calls=%fused_computation.38 | convolution fusion | flops 2768240640 | bytes 9519104 | tf_op jit(solution)/shard_map/secd,efd->secf/dot_general | solution.py:50
  155.2 5.3 %fusion.5 = (bf16[16,1,60,704]{3,2,0,1:T(8,128)(2,1)S(1)}, f32[16,60,704]{2,1,0:T(8,128)}) fusion(f32[16,60,704]{2,1,0:T(8,128)S(1)} %fusion.22, bf16[16,60,2048]{2,1,0:T(8,128)(2,1)S(1)} %copy-done.1, bf16[1,704,2048]{2,1,0:T(8,128)(2,1)S(1)} %copy-done.6), kind=kOutput, calls=%fused_computation.14 | convolution fusion | flops 2772295680 | bytes 13574144 | tf_op jit(solution)/shard_map/secd,efd->secf/dot_general | solution.py:51
  160.6 1.1 copy-done.7
  161.7 5.0 %convert_bitcast_fusion = bf16[16,1,60,2048]{3,2,0,1:T(8,128)(2,1)} fusion(bf16[1,704,2048]{2,1,0:T(8,128)(2,1)S(1)} %copy-done, bf16[16,1,60,704]{3,2,0,1:T(8,128)(2,1)S(1)} %get-tuple-element.6), kind=kOutput, calls=%fused_computation.4 | convolution fusion | flops 2770206720 | bytes 8167424 | tf_op jit(solution)/shard_map/secf,efd->secd/dot_general | solution.py:54
  166.7 0.0 reduce-scatter.2.cloned.1.call-update
  166.7 0.0 all-gather.5.cloned.1.call-done
  166.7 4.9 %reshape.138 = bf16[16,60,2048]{2,1,0:T(8,128)(2,1)} reshape(bf16[960,2048]{1,0:T(8,128)(2,1)} %all-gather.5.cloned.1.call-done) | data formatting | bytes 7864320 | tf_op jit(solution)/shard_map/reshape.23
  171.6 8.2 %fusion.16 = bf16[1,704,2048]{2,1,0:T(8,128)(2,1)} fusion(bf16[16,60,2048]{2,1,0:T(8,128)(2,1)} %reshape.138, bf16[16,1,60,704]{3,2,0,1:T(8,128)(2,1)} %copy-done.7), kind=kOutput, calls=%fused_computation.32 | convolution fusion | flops 2769682432 | bytes 8167424 | tf_op jit(solution)/shard_map/secf,secd->efd/dot_general | solution.py:68
  179.8 4.7 %all-to-all-start.1 = ((bf16[16,1,60,1024]{3,2,1,0:T(8,128)(2,1)}), bf16[16,1,60,1024]{3,2,1,0:T(8,128)(2,1)}, u32[]{:S(2)}, u32[]{:S(2)}) async-start(bf16[16,1,60,1024]{3,2,1,0:T(8,128)(2,1)} %bitcast.158), calls=%async_computation.2 | async-start | bytes 4194304 | tf_op jit(solution)/shard_map/all_to_all | solution.py:58
  184.5 5.5 %fusion.17 = f32[16,60,704]{2,1,0:T(8,128)S(1)} fusion(bf16[16,60,2048]{2,1,0:T(8,128)(2,1)} %reshape.138, bf16[1,704,2048]{2,1,0:T(8,128)(2,1)S(1)} %copy-done), kind=kOutput, calls=%fused_computation.33 | convolution fusion | flops 2768240640 | bytes 9519104 | tf_op jit(solution)/shard_map/secd,efd->secf/dot_general | solution.py:63
  190.1 4.8 %fusion.15 = bf16[1,704,2048]{2,1,0:T(8,128)(2,1)} fusion(bf16[16,60,2048]{2,1,0:T(8,128)(2,1)S(1)} %copy-done.2, f32[16,60,704]{2,1,0:T(8,128)S(1)} %fusion.17, f32[16,60,704]{2,1,0:T(8,128)S(1)} %copy-done.9), kind=kOutput, calls=%fused_computation.31 | convolution fusion | flops 2773737472 | bytes 12222464 | tf_op jit(solution)/shard_map/secf,secd->efd/dot_general | solution.py:74
  194.8 5.7 %fusion.14 = bf16[1,704,2048]{2,1,0:T(8,128)(2,1)} fusion(bf16[16,60,2048]{2,1,0:T(8,128)(2,1)S(1)} %copy-done.2, f32[16,60,704]{2,1,0:T(8,128)S(1)} %fusion.17, f32[16,60,704]{2,1,0:T(8,128)S(1)} %copy-done.10, f32[16,60,704]{2,1,0:T(8,128)S(1)} %copy-done.9), kind=kOutput, calls=%fused_computation.30 | convolution fusion | flops 2776440832 | bytes 14925824 | tf_op jit(solution)/shard_map/secf,secd->efd/dot_general | solution.py:71
  200.5 26.8 %all-to-all-done.1 = bf16[16,1,60,1024]{3,2,1,0:T(8,128)(2,1)} async-done(((bf16[16,1,60,1024]{3,2,1,0:T(8,128)(2,1)}), bf16[16,1,60,1024]{3,2,1,0:T(8,128)(2,1)}, u32[]{:S(2)}, u32[]{:S(2)}) %all-to-all-start.1) | async-done | bytes 1966112 | tf_op jit(solution)/shard_map/all_to_all | solution.py:58
  227.3 3.6 %reshape.153 = bf16[960,1024,1]{1,0,2:T(8,128)(2,1)} reshape(bf16[16,1,60,1024]{3,2,1,0:T(8,128)(2,1)} %all-to-all-done.1) | data formatting | bytes 3932160 | tf_op jit(solution)/shard_map/reshape | solution.py:58
  230.9 4.2 %multiply_reduce_fusion = bf16[128,1024]{1,0:T(8,128)(2,1)} fusion(f32[128,6]{0,1:T(8,128)S(1)} %copy-done.4, bf16[960,1024,1]{1,0,2:T(8,128)(2,1)} %reshape.153, s32[128,6]{0,1:T(8,128)S(1)} %multiply_add_fusion.1), kind=kOutput, calls=%fused_computation.22 | convolution fusion | flops 1512128512 | bytes 2234368 | tf_op jit(solution)/shard_map/skp,pd->skd/dot_general | solution.py:61
  (29 shorter events, 0.1 us)
Async XLA Ops:
  7.2 154.5 %copy-start = (bf16[1,704,2048]{2,1,0:T(8,128)(2,1)S(1)}, bf16[1,704,2048]{2,1,0:T(8,128)(2,1)}, u32[]{:S(2)}) copy-start(bf16[1,704,2048]{2,1,0:T(8,128)(2,1)} %param.17) | copy-start | bytes 8650756
  16.6 12.2 %copy-start.5 = (bf16[1024]{0:T(1024)(128)(2,1)S(1)}, bf16[1024]{0:T(1024)(128)(2,1)}, u32[]{:S(2)}) copy-start(bf16[1024]{0:T(1024)(128)(2,1)} %param.11) | copy-start | bytes 6148
  20.2 11.5 %copy-start.4 = (f32[128,6]{0,1:T(8,128)S(1)}, f32[128,6]{0,1:T(8,128)}, u32[]{:S(2)}) copy-start(f32[128,6]{0,1:T(8,128)} %param.13) | copy-start | bytes 9220
  20.2 51.6 %all-to-all-start = ((bf16[16,60,1024]{2,1,0:T(8,128)(2,1)}), bf16[16,60,1024]{2,1,0:T(8,128)(2,1)}, u32[]{:S(2)}, u32[]{:S(2)}) async-start(bf16[16,60,1024]{2,1,0:T(8,128)(2,1)} %all_to_all.19), calls=%async_computation | async-start | bytes 4194304 | tf_op jit(solution)/shard_map/all_to_all | solution.py:40
  28.7 114.5 %all-gather.3.cloned.1.call-start = ((), (), s32[]{:S(2)}) async-start(), calls=%async_computation.4 | async-start | bytes 5898240 | tf_op jit(solution)/shard_map/all_gather | solution.py:44
  29.0 46.5 %copy-start.3 = (bf16[128,1024]{1,0:T(8,128)(2,1)S(1)}, bf16[128,1024]{1,0:T(8,128)(2,1)}, u32[]{:S(2)}) copy-start(bf16[128,1024]{1,0:T(8,128)(2,1)} %param.14) | copy-start | bytes 786436
  75.5 91.3 %all-gather.5.cloned.1.call-start = ((), (), s32[]{:S(2)}) async-start(), calls=%async_computation.6 | async-start | bytes 5898240 | tf_op jit(solution)/shard_map/all_gather | solution.py:45
  142.9 36.9 %reduce-scatter.2.cloned.1.call-start = ((), (), s32[]{:S(2)}) async-start(), calls=%async_computation.5 | async-start | bytes 6291456 | tf_op jit(solution)/shard_map/reduce_scatter | solution.py:55
  148.1 7.1 %copy-start.1 = (bf16[16,60,2048]{2,1,0:T(8,128)(2,1)S(1)}, bf16[16,60,2048]{2,1,0:T(8,128)(2,1)}, u32[]{:S(2)}) copy-start(bf16[16,60,2048]{2,1,0:T(8,128)(2,1)} %reshape.132) | copy-start | bytes 11796484
  148.1 7.1 %copy-start.6 = (bf16[1,704,2048]{2,1,0:T(8,128)(2,1)S(1)}, bf16[1,704,2048]{2,1,0:T(8,128)(2,1)}, u32[]{:S(2)}) copy-start(bf16[1,704,2048]{2,1,0:T(8,128)(2,1)} %param.16) | copy-start | bytes 8650756
  155.2 5.4 %copy-start.8 = (f32[16,60,704]{2,1,0:T(8,128)}, f32[16,60,704]{2,1,0:T(8,128)S(1)}, u32[]{:S(2)}) copy-start(f32[16,60,704]{2,1,0:T(8,128)S(1)} %fusion.22) | copy-start | bytes 8110084
  160.6 1.1 copy-start.7
  179.8 47.5 %all-to-all-start.1 = ((bf16[16,1,60,1024]{3,2,1,0:T(8,128)(2,1)}), bf16[16,1,60,1024]{3,2,1,0:T(8,128)(2,1)}, u32[]{:S(2)}, u32[]{:S(2)}) async-start(bf16[16,1,60,1024]{3,2,1,0:T(8,128)(2,1)} %bitcast.158), calls=%async_computation.2 | async-start | bytes 4194304 | tf_op jit(solution)/shard_map/all_to_all | solution.py:58
  184.5 5.5 %copy-start.2 = (bf16[16,60,2048]{2,1,0:T(8,128)(2,1)S(1)}, bf16[16,60,2048]{2,1,0:T(8,128)(2,1)}, u32[]{:S(2)}) copy-start(bf16[16,60,2048]{2,1,0:T(8,128)(2,1)} %reshape.132) | copy-start | bytes 11796484
  184.5 5.5 %copy-start.9 = (f32[16,60,704]{2,1,0:T(8,128)S(1)}, f32[16,60,704]{2,1,0:T(8,128)}, u32[]{:S(2)}) copy-start(f32[16,60,704]{2,1,0:T(8,128)} %copy-done.8) | copy-start | bytes 8110084
  190.0 4.8 %copy-start.10 = (f32[16,60,704]{2,1,0:T(8,128)S(1)}, f32[16,60,704]{2,1,0:T(8,128)}, u32[]{:S(2)}) copy-start(f32[16,60,704]{2,1,0:T(8,128)} %get-tuple-element.7) | copy-start | bytes 8110084
Sparse Core Ops, SparseCore 0:
  75.6 17.6 all-gather.2
  143.1 11.5 all-gather.4
  166.8 10.1 reduce-scatter.1
where the time goes:
time: 247 us; the launch traced here: 242 us
  waiting for transfers between devices  66.4 us (27%)
  blocking collectives  60.9 us (25%)
  matrix products  49.9 us (20%)
  local copies, waits for them, and re-layouts  33 us (13%)
  between operations  14 us (6%)
  starting transfers between devices  13.5 us (5%)
  other arithmetic  3.97 us (2%)
    all_to_all x1, blocking collectives, local(): lax.all_to_all(cot_send, 'dp', split_axis=0, concat_axis=0, tiled=True)  58.3 us
    all_to_all x1, waiting for transfers between devices, local(): lax.all_to_all(token_send, 'dp', split_axis=0, concat_axis=0, tiled=True)  39.5 us
    all_to_all x1, waiting for transfers between devices, local(): lax.all_to_all(summed, 'dp', split_axis=0, concat_axis=0, tiled=True)  26.8 us
    another operation x2, local copies, waits for them, and re-layouts  9.77 us
    all_to_all x1, starting transfers between devices, local(): lax.all_to_all(token_send, 'dp', split_axis=0, concat_axis=0, tiled=True)  8.53 us
    dot_general x1, matrix products, local(): jnp.einsum('secf,secd->efd', hidden, cot_rows, preferred_element_type=jnp...  8.23 us
    all_to_all x2, local copies, waits for them, and re-layouts, local(): lax.all_to_all(token_send, 'dp', split_axis=0, concat_axis=0, tiled=True)  7.18 us
    all_to_all x2, local copies, waits for them, and re-layouts, local(): lax.all_to_all(cot_send, 'dp', split_axis=0, concat_axis=0, tiled=True)  7.17 us
  transfers between devices with their start and end apart: 5, of which 2 were waited for; matrix products, arithmetic and copies ran while one was open for 22% of the time, Pallas kernels for 0%

commit v1 on v0

--- a/solution.py
+++ b/solution.py
@@ -1,14 +1,22 @@
+import functools
 import jax
 import jax.numpy as jnp
 from jax import lax
+from jax.experimental import pallas as pl
+from jax.experimental.pallas import tpu as pltpu
 from jax.sharding import PartitionSpec as P
+
+MESH = pl.DeviceIdType.MESH
+PLANE = 4
+F32 = jnp.float32
+BF16 = jnp.bfloat16
 
 
 def slot_factor(route_hit, weights):
     return jnp.sum(jnp.where(route_hit, weights.reshape(-1)[:, None], 0.0), axis=0)
 
 
-def local(pool, select, reward_w, routes, gates, target, w_gate, w_up, w_down):
+def generic(pool, select, reward_w, routes, gates, target, w_gate, w_up, w_down):
     pool_rows = pool.shape[0]
     local_rows = select - lax.axis_index("dp") * pool_rows
     chosen = jnp.take(pool, local_rows, axis=0)
@@ -77,22 +85,431 @@
     return (mixed, grad_gate, grad_up, grad_down)
 
 
+def place(line):
+    d = lax.axis_index("dp")
+    c = lax.axis_index("tensor")
+    z, q = d // PLANE, d % PLANE
+    y, x = q // 2, q % 2
+    mates = [((y + ry) % 2) * 2 + (x + rx) % 2 for ry, rx in ((0, 1), (1, 0), (1, 1))]
+    return d, c, z, q, mates
+
+
+def greet(d, c, z, q, mates, line):
+    barrier = pltpu.get_barrier_semaphore()
+    for m in mates:
+        pl.semaphore_signal(barrier, inc=1, device_id=(z * PLANE + m, c), device_id_type=MESH)
+    pl.semaphore_signal(barrier, inc=1, device_id=(d, 1 - c), device_id_type=MESH)
+
+    @pl.when(z > 0)
+    def _():
+        pl.semaphore_signal(barrier, inc=1, device_id=(d - PLANE, c), device_id_type=MESH)
+
+    @pl.when(z < line - 1)
+    def _():
+        pl.semaphore_signal(barrier, inc=1, device_id=(d + PLANE, c), device_id_type=MESH)
+
+    below, above = (z + line - 1) // line, (2 * line - 2 - z) // line
+    pl.semaphore_wait(barrier, 4 + below + above)
+
+
+def remote(src, dst, send, recv, dev):
+    return pltpu.make_async_remote_copy(
+        src_ref=src, dst_ref=dst, send_sem=send, recv_sem=recv, device_id=dev, device_id_type=MESH
+    )
+
+
+def dispatch_kernel(
+    line, pad, pool_ref, sel_ref, rw_ref, rt_ref, gt_ref, target_ref,
+    rows0_ref, rows1_ref, side_ref,
+    data, scale, part, part_in, stage,
+    zsend, zrecv, ssend, srecv, csend, crecv, xsend, xrecv, tsend, trecv, psend, precv,
+):
+    d, c, z, q, mates = place(line)
+    experts = line * PLANE
+    sel_rows, half = target_ref.shape
+    top = gt_ref.shape[0]
+    rows = (rows0_ref, rows1_ref)
+    mine = pl.ds(pl.multiple_of(c * half, half), half)
+
+    hit = (
+        lax.broadcasted_iota(jnp.int32, (sel_rows, pool_ref.shape[0]), 1) == sel_ref[...]
+    ).astype(F32).astype(BF16)
+    chosen = jnp.dot(hit, pool_ref[...], preferred_element_type=F32).astype(BF16)
+    data[0, z] = chosen
+    data[1, z] = target_ref[...]
+    part[...] = lax.dot_general(
+        rw_ref[...], chosen, (((1,), (1,)), ((), ())), preferred_element_type=F32
+    )
+    expert_id = lax.broadcasted_iota(jnp.int32, (experts, sel_rows), 0)
+    member = jnp.zeros((experts, sel_rows), F32)
+    gate = jnp.zeros((experts, sel_rows), F32)
+    for k in range(top):
+        eq = rt_ref[k : k + 1, :] == expert_id
+        member = member + jnp.where(eq, 1.0, 0.0)
+        gate = gate + jnp.where(eq, gt_ref[k : k + 1, :], 0.0)
+    tri = jnp.where(
+        lax.broadcasted_iota(jnp.int32, (sel_rows, sel_rows), 0)
+        < lax.broadcasted_iota(jnp.int32, (sel_rows, sel_rows), 1),
+        1.0,
+        0.0,
+    ).astype(BF16)
+    before = jnp.dot(member.astype(BF16), tri, preferred_element_type=F32)
+    side_ref[z, 0:experts, :] = jnp.where(member > 0.5, before, -1.0)
+    side_ref[z, experts : 2 * experts, :] = gate
+
+    greet(d, c, z, q, mates, line)
+    partner = (d, 1 - c)
+    reward_copy = remote(part, part_in, psend, precv, partner)
+    reward_copy.start()
+
+    def zcopies(a, s, way):
+        blk = z - way * s
+        dev = (d + way * PLANE, c)
+        w = (way + 1) // 2
+        main = remote(data.at[a, blk], data.at[a, blk], zsend.at[a, w, s], zrecv.at[a, blk], dev)
+        if a == 0:
+            extra = remote(
+                side_ref.at[blk], side_ref.at[blk], ssend.at[w, s], srecv.at[blk], dev
+            )
+        else:
+            extra = remote(scale.at[blk], scale.at[blk], csend.at[w, s], crecv.at[blk], dev)
+        return extra, main
+
+    def sends(a, s, way):
+        blk, to = z - way * s, z + way
+        return (blk >= 0) & (blk < line) & (to >= 0) & (to < line)
+
+    def zstart(a, s):
+        for way in (1, -1):
+            @pl.when(sends(a, s, way))
+            def _():
+                for cp in zcopies(a, s, way):
+                    cp.start()
+
+    def arrives(s, way):
+        blk = z - way * (s + 1)
+        return (blk >= 0) & (blk < line)
+
+    def zwait(a, s):
+        for way in (1, -1):
+            @pl.when(arrives(s, way))
+            def _():
+                blk = z - way * (s + 1)
+                dev = (d, 1 - c)
+                remote(
+                    data.at[a, blk], data.at[a, blk], zsend.at[a, 0, 0], zrecv.at[a, blk], dev
+                ).wait_recv()
+                if a == 0:
+                    remote(
+                        side_ref.at[blk], side_ref.at[blk], ssend.at[0, 0], srecv.at[blk], dev
+                    ).wait_recv()
+                else:
+                    remote(
+                        scale.at[blk], scale.at[blk], csend.at[0, 0], crecv.at[blk], dev
+                    ).wait_recv()
+
+    def tcopy(a, b):
+        place_ = rows[a].at[b, :, mine]
+        return remote(place_, place_, tsend.at[a, b], trecv.at[a, b], partner)
+
+    def xcopy(a, zp, r):
+        return remote(
+            stage.at[a, zp, r],
+            rows[a].at[zp * PLANE + q, :, mine],
+            xsend.at[a, zp, r],
+            xrecv.at[a, zp * PLANE + q],
+            (z * PLANE + mates[r], c),
+        )
+
+    slot_id = lax.broadcasted_iota(jnp.int32, (pad, sel_rows), 0).astype(F32)
+
+    def process(a, zp):
+        block = data[a, zp]
+        for r in (0, 1, 2, 3):
+            e = z * PLANE + (mates[r] if r < 3 else q)
+            m = slot_id == side_ref[zp, pl.ds(e, 1), :]
+            picked = jnp.dot(
+                jnp.where(m, 1.0, 0.0).astype(BF16), block, preferred_element_type=F32
+            )
+            if a == 1:
+                picked = picked * jnp.sum(
+                    jnp.where(m, scale[zp, pl.ds(e, 1), :], 0.0), axis=1, keepdims=True
+                )
+            picked = picked.astype(BF16)
+            if r < 3:
+                stage[a, zp, r] = picked
+                xcopy(a, zp, r).start()
+            else:
+                rows[a][zp * PLANE + q, :, mine] = picked
+                tcopy(a, zp * PLANE + q).start()
+
+    def forward(a, zp):
+        for r in range(3):
+            b = zp * PLANE + mates[r]
+            remote(
+                stage.at[a, zp, r], rows[a].at[b, :, mine], xsend.at[a, zp, r],
+                xrecv.at[a, b], partner,
+            ).wait_recv()
+            tcopy(a, b).start()
+
+    def got(fn, a, s):
+        for way in (1, -1):
+            @pl.when(arrives(s, way))
+            def _():
+                fn(a, z - way * (s + 1))
+
+    zstart(0, 0)
+    process(0, z)
+    reward_copy.wait()
+    keep = 1.0 / (1.0 + jnp.exp(-(part[0:1, :] + part_in[0:1, :])))
+    scale[z] = keep * side_ref[z, experts : 2 * experts, :]
+    last = line - 2
+    for a in (0, 1):
+        for s in range(line - 1):
+            zwait(a, s)
+            if s < last:
+                zstart(a, s + 1)
+            elif a == 0:
+                zstart(1, 0)
+            got(process, a, s)
+            if s == 0:
+                forward(a, z)
+            else:
+                got(forward, a, s - 1)
+        if a == 0:
+            process(1, z)
+        got(forward, a, last)
+
+    for a in (0, 1):
+        for b in range(experts):
+            tcopy(a, b).wait()
+        for zp in range(line):
+            for r in range(3):
+                xcopy(a, zp, r).wait_send()
+        for s in range(line - 1):
+            for way in (1, -1):
+                @pl.when(sends(a, s, way))
+                def _():
+                    for cp in zcopies(a, s, way):
+                        cp.wait_send()
+
+
+def return_kernel(
+    line, pad, value_ref, side_ref, mixed_ref,
+    partner_in, stage, plane_in, acc, out_stage, line_in,
+    tsend, trecv, xsend, xrecv, zsend, zrecv,
+):
+    d, c, z, q, mates = place(line)
+    experts = line * PLANE
+    half = mixed_ref.shape[1]
+    sel_rows = mixed_ref.shape[0]
+    mine = pl.ds(pl.multiple_of(c * half, half), half)
+    other = pl.ds(pl.multiple_of((1 - c) * half, half), half)
+    partner = (d, 1 - c)
+    turn = 2 * (z // (line // 2)) - 1
+
+    def order(i):
+        return (z + turn * (1 + i) + 2 * line) % line
+
+    greet(d, c, z, q, mates, line)
+
+    def tcopy(b):
+        return remote(
+            value_ref.at[b, :, other], partner_in.at[b], tsend.at[b], trecv.at[b], partner
+        )
+
+    def xcopy(zp, r):
+        return remote(
+            stage.at[zp, r], plane_in.at[zp, q], xsend.at[zp, r], xrecv.at[zp, q],
+            (z * PLANE + mates[r], c),
+        )
+
+    for i in range(line):
+        for r in (2, 0, 1, 3):
+            tcopy(order(i) * PLANE + (mates[r] if r < 3 else q)).start()
+    for i in range(line):
+        zp = order(i)
+        for r in (2, 0, 1, 3):
+            b = zp * PLANE + (mates[r] if r < 3 else q)
+            tcopy(b).wait_recv()
+            total = (value_ref[b, :, mine].astype(F32) + partner_in[b].astype(F32)).astype(BF16)
+            if r < 3:
+                stage[zp, r] = total
+                xcopy(zp, r).start()
+            else:
+                plane_in[zp, q] = total
+
+    slot_id = lax.broadcasted_iota(jnp.int32, (pad, sel_rows), 0).astype(F32)
+
+    def combine(zp):
+        for r in range(3):
+            remote(
+                stage.at[zp, r], plane_in.at[zp, mates[r]], xsend.at[zp, r],
+                xrecv.at[zp, mates[r]], partner,
+            ).wait_recv()
+        total = jnp.zeros((sel_rows, half), F32)
+        for j in range(PLANE):
+            e = z * PLANE + j
+            w = jnp.where(
+                slot_id == side_ref[zp, pl.ds(e, 1), :],
+                side_ref[zp, pl.ds(experts + e, 1), :],
+                0.0,
+            )
+            high = w.astype(BF16)
+            low = (w - high.astype(F32)).astype(BF16)
+            both = jnp.concatenate([high, low], axis=0)
+            values = plane_in[zp, j]
+            total = total + lax.dot_general(
+                both, jnp.concatenate([values, values], axis=0),
+                (((0,), (0,)), ((), ())), preferred_element_type=F32,
+            )
+        acc[zp] = total
+
+    def zcopy(w, s):
+        to = d + (2 * w - 1) * PLANE
+        return remote(
+            out_stage.at[w, s], line_in.at[w, s], zsend.at[w, s], zrecv.at[w, s], (to, c)
+        )
+
+    def height(w):
+        return z if w == 1 else line - 1 - z
+
+    def sends(w, s):
+        return (height(w) <= s) & (height(w) < line - 1)
+
+    def arrives(w, s):
+        return (height(w) > 0) & (height(w) - 1 <= s)
+
+    for s in range(line - 1):
+        combine(order(s))
+        if s > 0:
+            for w in (1, 0):
+                @pl.when(arrives(w, s - 1))
+                def _():
+                    zcopy(w, s - 1).wait_recv()
+        for w in (1, 0):
+            blk = z + (2 * w - 1) * (line - 1 - s)
+
+            @pl.when(sends(w, s) & (height(w) > 0))
+            def _():
+                if s > 0:
+                    out_stage[w, s] = (acc[blk] + line_in[w, s - 1].astype(F32)).astype(BF16)
+                    zcopy(w, s).start()
+
+            @pl.when(sends(w, s) & (height(w) == 0))
+            def _():
+                out_stage[w, s] = acc[blk].astype(BF16)
+                zcopy(w, s).start()
+    combine(z)
+    final = line - 2
+    for w in (1, 0):
+        @pl.when(arrives(w, final))
+        def _():
+            zcopy(w, final).wait_recv()
+            acc[z] = acc[z] + line_in[w, final].astype(F32)
+    mixed_ref[...] = acc[z].astype(BF16)
+
+    for b in range(experts):
+        tcopy(b).wait_send()
+    for zp in range(line):
+        for r in range(3):
+            xcopy(zp, r).wait_send()
+    for s in range(line - 1):
+        for w in (1, 0):
+            @pl.when(sends(w, s))
+            def _():
+                zcopy(w, s).wait_send()
+
+
+def vmem(count):
+    return [pl.BlockSpec(memory_space=pltpu.VMEM)] * count
+
+
+DMA = pltpu.SemaphoreType.DMA
+
+
+def planar(pool, select, reward_w, routes, gates, target, w_gate, w_up, w_down):
+    dp = lax.axis_size("dp")
+    line = dp // PLANE
+    experts = dp * w_gate.shape[0]
+    sel_rows, top = routes.shape
+    capacity = 5 * sel_rows * top // (4 * experts)
+    pad = -(-capacity // 16) * 16
+    half = target.shape[1]
+    width = w_gate.shape[2]
+    sel = (select - lax.axis_index("dp") * pool.shape[0]).reshape(sel_rows, 1)
+    rw = jnp.broadcast_to(reward_w[None, :], (16, half))
+    rows_shape = jax.ShapeDtypeStruct((experts, pad, width), BF16)
+    tokens, cots, side = pl.pallas_call(
+        functools.partial(dispatch_kernel, line, pad),
+        name="dispatch",
+        out_shape=(
+            rows_shape, rows_shape, jax.ShapeDtypeStruct((line, 2 * experts, sel_rows), F32)
+        ),
+        in_specs=vmem(6),
+        out_specs=tuple(vmem(3)),
+        scratch_shapes=[
+            pltpu.VMEM((2, line, sel_rows, half), BF16),
+            pltpu.VMEM((line, experts, sel_rows), F32),
+            pltpu.VMEM((16, sel_rows), F32),
+            pltpu.VMEM((16, sel_rows), F32),
+            pltpu.VMEM((2, line, 3, pad, half), BF16),
+            DMA((2, 2, line)), DMA((2, line)), DMA((2, line)), DMA((line,)),
+            DMA((2, line)), DMA((line,)), DMA((2, line, 3)), DMA((2, experts)),
+            DMA((2, experts)), DMA((2, experts)), DMA, DMA,
+        ],
+        compiler_params=pltpu.CompilerParams(
+            collective_id=0, has_side_effects=True, vmem_limit_bytes=50 * 2**20
+        ),
+    )(pool, sel, rw, routes.T, gates.T, target)
+    token_rows = tokens.reshape(experts * pad, width)
+    cot_rows = cots.reshape(experts * pad, width)
+    wg, wu, wd = w_gate[0], w_up[0], w_down[0]
+    dot = functools.partial(jnp.einsum, preferred_element_type=F32)
+    gate_act = dot("rd,fd->rf", token_rows, wg)
+    up_act = dot("rd,fd->rf", token_rows, wu)
+    sig = jax.nn.sigmoid(gate_act)
+    hidden = (gate_act * sig * up_act).astype(BF16)
+    value = dot("rf,fd->rd", hidden, wd).astype(BF16).reshape(experts, pad, width)
+    mixed = pl.pallas_call(
+        functools.partial(return_kernel, line, pad),
+        name="give_back",
+        out_shape=jax.ShapeDtypeStruct((sel_rows, half), BF16),
+        in_specs=vmem(2),
+        out_specs=vmem(1)[0],
+        scratch_shapes=[
+            pltpu.VMEM((experts, pad, half), BF16),
+            pltpu.VMEM((line, 3, pad, half), BF16),
+            pltpu.VMEM((line, PLANE, pad, half), BF16),
+            pltpu.VMEM((line, sel_rows, half), F32),
+            pltpu.VMEM((2, line, sel_rows, half), BF16),
+            pltpu.VMEM((2, line, sel_rows, half), BF16),
+            DMA((experts,)), DMA((experts,)), DMA((line, 3)), DMA((line, PLANE)),
+            DMA((2, line)), DMA((2, line)),
+        ],
+        compiler_params=pltpu.CompilerParams(
+            collective_id=1, has_side_effects=True, vmem_limit_bytes=50 * 2**20
+        ),
+    )(value, side)
+    hidden_grad = dot("rd,fd->rf", cot_rows, wd)
+    gate_grad = (hidden_grad * up_act * sig * (1.0 + gate_act * (1.0 - sig))).astype(BF16)
+    up_grad = (hidden_grad * gate_act * sig).astype(BF16)
+    grad_down = dot("rf,rd->fd", hidden, cot_rows).astype(BF16)[None]
+    grad_gate = dot("rf,rd->fd", gate_grad, token_rows).astype(BF16)[None]
+    grad_up = dot("rf,rd->fd", up_grad, token_rows).astype(BF16)[None]
+    return mixed, grad_gate, grad_up, grad_down
+
+
 def solution(mesh):
     in_specs = (
-        P("dp", "tensor"),
-        P("dp"),
-        P("tensor"),
-        P("dp", None),
-        P("dp", None),
-        P("dp", "tensor"),
+        P("dp", "tensor"), P("dp"), P("tensor"), P("dp", None), P("dp", None), P("dp", "tensor"),
+        P("dp", "tensor", None), P("dp", "tensor", None), P("dp", "tensor", None),
+    )
+    out_specs = (
+        P("dp", "tensor"), P("dp", "tensor", None), P("dp", "tensor", None),
         P("dp", "tensor", None),
-        P("dp", "tensor", None),
-        P("dp", "tensor", None),
-    )
-    out_specs = (
-        P("dp", "tensor"),
-        P("dp", "tensor", None),
-        P("dp", "tensor", None),
-        P("dp", "tensor", None),
-    )
+    )
+    dp, tensor = mesh.shape["dp"], mesh.shape["tensor"]
+    fits = tensor == 2 and dp % (2 * PLANE) == 0
+    local = planar if fits else generic
     return jax.shard_map(local, mesh=mesh, in_specs=in_specs, out_specs=out_specs, check_vma=False)

time: 247 us -> 134 us (0.54); the launches traced: 242 us -> 133 us
  Pallas kernels: 0 us -> 95 us
  waiting for transfers between devices: 66.4 us -> 0 us
  blocking collectives: 60.9 us -> 0 us
  local copies, waits for them, and re-layouts: 33 us -> 4.89 us
  matrix products: 49.9 us -> 31.9 us
  starting transfers between devices: 13.5 us -> 0 us
  between operations: 14 us -> 0.74 us
  other arithmetic: 3.97 us -> 0.81 us
    pallas_call x0 -> x2, Pallas kernels: none -> 95 us  [the longest x1 61.7 us: planar(): pl.pallas_call(functools.partial(dispatch_kernel, line, pad), name='dispa...]
    all_to_all x2 -> x0, waiting for transfers between devices: 66.3 us -> none  [the longest x1 39.5 us: local(): lax.all_to_all(token_send, 'dp', split_axis=0, concat_axis=0, tiled=True)]
    all_to_all x1 -> x0, blocking collectives: 58.3 us -> none  [local(): lax.all_to_all(cot_send, 'dp', split_axis=0, concat_axis=0, tiled=True)]
    dot_general x11 -> x7, matrix products: 49.9 us -> 31.9 us  [the longest x1 6.01 us: planar(): gate_act = dot('rd,fd->rf', token_rows, wg)]
    all_to_all x4 -> x0, local copies, waits for them, and re-layouts: 14.3 us -> none  [the longest x2 7.18 us: local(): lax.all_to_all(token_send, 'dp', split_axis=0, concat_axis=0, tiled=True)]
    all_to_all x2 -> x0, starting transfers between devices: 13.2 us -> none  [the longest x1 8.53 us: local(): lax.all_to_all(token_send, 'dp', split_axis=0, concat_axis=0, tiled=True)]
    another operation x2 -> x0, local copies, waits for them, and re-layouts: 9.77 us -> none
    reshape x1, local copies, waits for them, and re-layouts: 3.61 us -> 0.12 us  [planar(): sel = (select - lax.axis_index('dp') * pool.shape[0]).reshape(sel_rows, 1)]
  transfers between devices with their start and end apart: 5 -> 0, of which waited for: 2 -> 0; matrix products, arithmetic and copies ran while one was open for 22% -> 0% of each run, Pallas kernels for 0% -> 0%
where the time goes in v1:
time: 134 us; the launch traced here: 133 us
  Pallas kernels  95 us (71%)
  matrix products  31.9 us (24%)
  local copies, waits for them, and re-layouts  4.89 us (4%)
    pallas_call x1, Pallas kernels, planar(): pl.pallas_call(functools.partial(dispatch_kernel, line, pad), name='dispa...  61.7 us
    pallas_call x1, Pallas kernels, planar(): pl.pallas_call(functools.partial(return_kernel, line, pad), name='give_ba...  33.3 us
    dot_general x1, matrix products, planar(): gate_act = dot('rd,fd->rf', token_rows, wg)  6.01 us
    dot_general x1, matrix products, planar(): grad_gate = dot('rf,rd->fd', gate_grad, token_rows).astype(BF16)[None]  5.34 us
    dot_general x1, matrix products, planar(): dot('rf,fd->rd', hidden, wd).astype(BF16).reshape(experts, pad, width)  5.03 us
    dot_general x1, matrix products, planar(): grad_up = dot('rf,rd->fd', up_grad, token_rows).astype(BF16)[None]  4.54 us
    dot_general x1, matrix products, planar(): grad_down = dot('rf,rd->fd', hidden, cot_rows).astype(BF16)[None]  4.43 us
    unnamed x17, local copies, waits for them, and re-layouts  4.09 us

profile of v1, /device:TPU:0, one launch (start us, length us, event | category | flops | bytes accessed | tf_op | source)
XLA Modules:
  0.0 133.4 jit_solution(2087543724236358056)
XLA Ops:
  0.6 0.0 copy-start
  0.7 0.8 subtract_bitcast_fusion
  1.5 0.1 copy.13.sel_ref
  1.6 0.7 broadcast_in_dim.15.rw_ref
  2.3 0.0 copy-start.1
  2.3 1.0 copy-done.1
  3.3 0.0 copy-start.2
  3.3 0.9 copy-done.2
  4.3 0.0 copy-start.3
  4.3 0.7 copy-done.3
  4.9 0.0 copy-start.4
  4.9 0.7 copy-done.4
  5.6 61.7 %dispatch.1 = (bf16[16,64,2048]{2,1,0:T(8,128)(2,1)}, bf16[16,64,2048]{2,1,0:T(8,128)(2,1)}, f32[4,32,128]{2,1,0:T(8,128)S(1)}) custom-call(bf16[256,1024]{1,0:T(8,128)(2,1)S(1)} %copy-done.1, s32[128,1]{1,0:T(8,128)S(1)} %copy.13.sel_ref, bf16[16,1024]{1,0:T(8,128)(2,1)S(1)} %broadcast_in_dim.15.rw_ref, s32[6,128]{1,0:T(8,128)S(1)} %bitcast.34, ...), custom_call_target="tpu_custom_call" | custom-call | tf_op jit(solution)/shard_map/dispatch/pallas_call | solution.py:443
  67.3 0.0 copy-start.5
  67.3 0.0 copy-start.7
  67.3 6.0 %fusion.8 = f32[1024,704]{0,1:T(8,128)S(1)} fusion(bf16[1024,2048]{1,0:T(8,128)(2,1)} %bitcast.37, bf16[1,704,2048]{2,1,0:T(8,128)(2,1)} %param.15), kind=kOutput, calls=%fused_computation.12 | convolution fusion | flops 2952790016 | bytes 9961472 | tf_op jit(solution)/shard_map/rd,fd->rf/dot_general | solution.py:469
  73.3 0.0 copy-done.5
  73.3 0.0 copy-done.7
  73.4 0.0 copy-start.6
  73.4 3.4 %multiply_convert_fusion.2 = (bf16[1024,704]{0,1:T(8,128)(2,1)S(1)}, f32[1024,704]{0,1:T(8,128)S(1)}) fusion(f32[1024,704]{0,1:T(8,128)S(1)} %fusion.8, bf16[1024,2048]{1,0:T(8,128)(2,1)S(1)} %bitcast.38, bf16[1,704,2048]{2,1,0:T(8,128)(2,1)S(1)} %copy-done.7), kind=kOutput, calls=%fused_computation.16 | convolution fusion | flops 2957115392 | bytes 14286848 | tf_op jit(solution)/shard_map/rd,fd->rf/dot_general | solution.py:470
  76.8 0.0 copy-done
  76.8 0.0 copy-done.6
  76.8 3.2 %fusion.3 = f32[1024,704]{0,1:T(8,128)S(1)} fusion(bf16[1024,2048]{1,0:T(8,128)(2,1)S(1)} %bitcast.41, bf16[1,704,2048]{2,1,0:T(8,128)(2,1)S(1)} %copy-done), kind=kOutput, calls=%fused_computation.7 | convolution fusion | flops 2952790016 | bytes 9961472 | tf_op jit(solution)/shard_map/rd,fd->rf/dot_general | solution.py:494
  80.0 5.3 %fusion = bf16[1,704,2048]{2,1,0:T(8,128)(2,1)} fusion(bf16[1024,2048]{1,0:T(8,128)(2,1)S(1)} %bitcast.39, f32[1024,704]{0,1:T(8,128)S(1)} %fusion.8, f32[1024,704]{0,1:T(8,128)S(1)} %fusion.3, f32[1024,704]{0,1:T(8,128)S(1)} %get-tuple-element.11), kind=kOutput, calls=%fused_computation.4 | convolution fusion | flops 2961440768 | bytes 15728640 | tf_op jit(solution)/shard_map/rf,rd->fd/dot_general | solution.py:498
  85.3 4.4 %fusion.2 = bf16[1,704,2048]{2,1,0:T(8,128)(2,1)} fusion(bf16[1024,704]{0,1:T(8,128)(2,1)S(1)} %get-tuple-element.10, bf16[1024,2048]{1,0:T(8,128)(2,1)S(1)} %bitcast.42), kind=kOutput, calls=%fused_computation.6 | convolution fusion | flops 2954231808 | bytes 8519680 | tf_op jit(solution)/shard_map/rf,rd->fd/dot_general | solution.py:497
  89.8 4.5 %fusion.1 = bf16[1,704,2048]{2,1,0:T(8,128)(2,1)} fusion(bf16[1024,2048]{1,0:T(8,128)(2,1)S(1)} %bitcast.40, f32[1024,704]{0,1:T(8,128)S(1)} %fusion.3, f32[1024,704]{0,1:T(8,128)S(1)} %fusion.8), kind=kOutput, calls=%fused_computation.5 | convolution fusion | flops 2958557184 | bytes 12845056 | tf_op jit(solution)/shard_map/rf,rd->fd/dot_general | solution.py:499
  94.3 5.0 %convolution_convert_fusion = bf16[1024,2048]{1,0:T(8,128)(2,1)} fusion(bf16[1024,704]{0,1:T(8,128)(2,1)S(1)} %get-tuple-element.10, bf16[1,704,2048]{2,1,0:T(8,128)(2,1)S(1)} %copy-done), kind=kOutput, calls=%fused_computation | convolution fusion | flops 2954887168 | bytes 8519680 | tf_op jit(solution)/shard_map/rf,fd->rd/dot_general | solution.py:473
  99.3 33.3 %give_back.1 = bf16[128,1024]{1,0:T(8,128)(2,1)S(1)} custom-call(bf16[16,64,2048]{2,1,0:T(8,128)(2,1)} %bitcast.36, f32[4,32,128]{2,1,0:T(8,128)S(1)} %get-tuple-element.8.side_ref), custom_call_target="tpu_custom_call" | custom-call | tf_op jit(solution)/shard_map/give_back/pallas_call | solution.py:474
  132.7 0.7 copy.15
Async XLA Ops:
  0.6 76.2 %copy-start = (bf16[1,704,2048]{2,1,0:T(8,128)(2,1)S(1)}, bf16[1,704,2048]{2,1,0:T(8,128)(2,1)}, u32[]{:S(2)}) copy-start(bf16[1,704,2048]{2,1,0:T(8,128)(2,1)} %param.17) | copy-start | bytes 8650756
  2.3 1.0 copy-start.1
  3.3 0.9 copy-start.2
  4.3 0.7 copy-start.3
  4.9 0.7 copy-start.4
  67.3 6.0 %copy-start.5 = (bf16[16,64,2048]{2,1,0:T(8,128)(2,1)S(1)}, bf16[16,64,2048]{2,1,0:T(8,128)(2,1)}, u32[]{:S(2)}) copy-start(bf16[16,64,2048]{2,1,0:T(8,128)(2,1)} %get-tuple-element.7) | copy-start | bytes 12582916
  67.3 6.0 %copy-start.7 = (bf16[1,704,2048]{2,1,0:T(8,128)(2,1)S(1)}, bf16[1,704,2048]{2,1,0:T(8,128)(2,1)}, u32[]{:S(2)}) copy-start(bf16[1,704,2048]{2,1,0:T(8,128)(2,1)} %param.16) | copy-start | bytes 8650756
  73.4 3.5 %copy-start.6 = (bf16[16,64,2048]{2,1,0:T(8,128)(2,1)S(1)}, bf16[16,64,2048]{2,1,0:T(8,128)(2,1)}, u32[]{:S(2)}) copy-start(bf16[16,64,2048]{2,1,0:T(8,128)(2,1)} %get-tuple-element.9) | copy-start | bytes 12582916

commit v2 on v1

--- a/solution.py
+++ b/solution.py
@@ -118,35 +118,51 @@
     )
 
 
-def dispatch_kernel(
-    line, pad, pool_ref, sel_ref, rw_ref, rt_ref, gt_ref, target_ref,
-    rows0_ref, rows1_ref, side_ref,
-    data, scale, part, part_in, stage,
-    zsend, zrecv, ssend, srecv, csend, crecv, xsend, xrecv, tsend, trecv, psend, precv,
+def layer_kernel(
+    line, pad, pool_hbm, sel_ref, rw_ref, rt_ref, gt_ref, target_hbm, wg_hbm, wu_hbm, wd_hbm,
+    mixed_ref, gg_hbm, gu_hbm, gd_hbm,
+    pool_ref, wide, wg, wu, wd, tok, cot, gate_act, up_act, hid, ggrad, ugrad, val,
+    data, side_ref, scale, part, part_in, stage,
+    partner_in, back, plane_in, acc, out_stage, line_in,
+    lsem, osem, zsend, zrecv, ssend, srecv, csend, crecv, xsend, xrecv, tsend, trecv, psend, precv,
+    vsend, vrecv, bsend, brecv, usend, urecv,
 ):
     d, c, z, q, mates = place(line)
     experts = line * PLANE
-    sel_rows, half = target_ref.shape
-    top = gt_ref.shape[0]
-    rows = (rows0_ref, rows1_ref)
+    sel_rows, half = mixed_ref.shape
+    top = gt_ref.shape[1]
+    units, width = wg.shape
+    span = PLANE * pad
+    rows = (tok, cot)
     mine = pl.ds(pl.multiple_of(c * half, half), half)
-
-    hit = (
-        lax.broadcasted_iota(jnp.int32, (sel_rows, pool_ref.shape[0]), 1) == sel_ref[...]
-    ).astype(F32).astype(BF16)
-    chosen = jnp.dot(hit, pool_ref[...], preferred_element_type=F32).astype(BF16)
-    data[0, z] = chosen
-    data[1, z] = target_ref[...]
-    part[...] = lax.dot_general(
-        rw_ref[...], chosen, (((1,), (1,)), ((), ())), preferred_element_type=F32
-    )
-    expert_id = lax.broadcasted_iota(jnp.int32, (experts, sel_rows), 0)
+    other = pl.ds(pl.multiple_of((1 - c) * half, half), half)
+    partner = (d, 1 - c)
+    turn = 2 * (z // (line // 2)) - 1
+
+    def order(i):
+        return (z + turn * (1 + i) + 2 * line) % line
+
+    loads = [
+        pltpu.make_async_copy(src, dst, lsem.at[i])
+        for i, (src, dst) in enumerate((
+            (pool_hbm, pool_ref), (target_hbm, data.at[1, z]), (wg_hbm.at[0], wg),
+            (wu_hbm.at[0], wu), (wd_hbm.at[0], wd),
+        ))
+    ]
+    for cp in loads:
+        cp.start()
+
+    wide[0, :, 0:top] = rt_ref[...].astype(F32)
+    wide[1, :, 0:top] = gt_ref[...]
+    routes_t = wide[0].T
+    gates_t = wide[1].T
+    expert_id = lax.broadcasted_iota(jnp.int32, (experts, sel_rows), 0).astype(F32)
     member = jnp.zeros((experts, sel_rows), F32)
     gate = jnp.zeros((experts, sel_rows), F32)
     for k in range(top):
-        eq = rt_ref[k : k + 1, :] == expert_id
+        eq = routes_t[k : k + 1, :] == expert_id
         member = member + jnp.where(eq, 1.0, 0.0)
-        gate = gate + jnp.where(eq, gt_ref[k : k + 1, :], 0.0)
+        gate = gate + jnp.where(eq, gates_t[k : k + 1, :], 0.0)
     tri = jnp.where(
         lax.broadcasted_iota(jnp.int32, (sel_rows, sel_rows), 0)
         < lax.broadcasted_iota(jnp.int32, (sel_rows, sel_rows), 1),
@@ -157,8 +173,21 @@
     side_ref[z, 0:experts, :] = jnp.where(member > 0.5, before, -1.0)
     side_ref[z, experts : 2 * experts, :] = gate
 
+    pool_rows = pool_ref.shape[0]
+    hit = (
+        lax.broadcasted_iota(jnp.int32, (pool_rows, sel_rows), 0) == sel_ref[...] - d * pool_rows
+    ).astype(F32).astype(BF16)
+    loads[0].wait()
+    chosen = lax.dot_general(
+        hit, pool_ref[...], (((0,), (0,)), ((), ())), preferred_element_type=F32
+    ).astype(BF16)
+    data[0, z] = chosen
+    part[...] = lax.dot_general(
+        jnp.broadcast_to(rw_ref[...].astype(F32), (16, half)).astype(BF16), chosen,
+        (((1,), (1,)), ((), ())), preferred_element_type=F32,
+    )
+
     greet(d, c, z, q, mates, line)
-    partner = (d, 1 - c)
     reward_copy = remote(part, part_in, psend, precv, partner)
     reward_copy.start()
 
@@ -195,22 +224,25 @@
             @pl.when(arrives(s, way))
             def _():
                 blk = z - way * (s + 1)
-                dev = (d, 1 - c)
                 remote(
-                    data.at[a, blk], data.at[a, blk], zsend.at[a, 0, 0], zrecv.at[a, blk], dev
+                    data.at[a, blk], data.at[a, blk], zsend.at[a, 0, 0], zrecv.at[a, blk], partner
                 ).wait_recv()
                 if a == 0:
                     remote(
-                        side_ref.at[blk], side_ref.at[blk], ssend.at[0, 0], srecv.at[blk], dev
+                        side_ref.at[blk], side_ref.at[blk], ssend.at[0, 0], srecv.at[blk], partner
                     ).wait_recv()
                 else:
                     remote(
-                        scale.at[blk], scale.at[blk], csend.at[0, 0], crecv.at[blk], dev
+                        scale.at[blk], scale.at[blk], csend.at[0, 0], crecv.at[blk], partner
                     ).wait_recv()
 
     def tcopy(a, b):
-        place_ = rows[a].at[b, :, mine]
-        return remote(place_, place_, tsend.at[a, b], trecv.at[a, b], partner)
+        spot = rows[a].at[b, :, mine]
+        return remote(spot, spot, tsend.at[a, b], trecv.at[a, b], partner)
+
+    def tarrive(a, b):
+        spot = rows[a].at[b, :, other]
+        remote(spot, spot, tsend.at[a, b], trecv.at[a, b], partner).wait_recv()
 
     def xcopy(a, zp, r):
         return remote(
@@ -225,7 +257,7 @@
 
     def process(a, zp):
         block = data[a, zp]
-        for r in (0, 1, 2, 3):
+        for r in (2, 0, 1, 3):
             e = z * PLANE + (mates[r] if r < 3 else q)
             m = slot_id == side_ref[zp, pl.ds(e, 1), :]
             picked = jnp.dot(
@@ -258,94 +290,86 @@
             def _():
                 fn(a, z - way * (s + 1))
 
-    zstart(0, 0)
-    process(0, z)
-    reward_copy.wait()
-    keep = 1.0 / (1.0 + jnp.exp(-(part[0:1, :] + part_in[0:1, :])))
-    scale[z] = keep * side_ref[z, experts : 2 * experts, :]
-    last = line - 2
-    for a in (0, 1):
-        for s in range(line - 1):
-            zwait(a, s)
-            if s < last:
-                zstart(a, s + 1)
-            elif a == 0:
-                zstart(1, 0)
-            got(process, a, s)
-            if s == 0:
-                forward(a, z)
-            else:
-                got(forward, a, s - 1)
-        if a == 0:
-            process(1, z)
-        got(forward, a, last)
-
-    for a in (0, 1):
-        for b in range(experts):
-            tcopy(a, b).wait()
-        for zp in range(line):
-            for r in range(3):
-                xcopy(a, zp, r).wait_send()
-        for s in range(line - 1):
-            for way in (1, -1):
-                @pl.when(sends(a, s, way))
-                def _():
-                    for cp in zcopies(a, s, way):
-                        cp.wait_send()
-
-
-def return_kernel(
-    line, pad, value_ref, side_ref, mixed_ref,
-    partner_in, stage, plane_in, acc, out_stage, line_in,
-    tsend, trecv, xsend, xrecv, zsend, zrecv,
-):
-    d, c, z, q, mates = place(line)
-    experts = line * PLANE
-    half = mixed_ref.shape[1]
-    sel_rows = mixed_ref.shape[0]
-    mine = pl.ds(pl.multiple_of(c * half, half), half)
-    other = pl.ds(pl.multiple_of((1 - c) * half, half), half)
-    partner = (d, 1 - c)
-    turn = 2 * (z // (line // 2)) - 1
-
-    def order(i):
-        return (z + turn * (1 + i) + 2 * line) % line
-
-    greet(d, c, z, q, mates, line)
-
-    def tcopy(b):
+    def vcopy(b):
+        return remote(val.at[b, :, other], partner_in.at[b], vsend.at[b], vrecv.at[b], partner)
+
+    def lanes(zp):
+        return pl.ds(pl.multiple_of(zp * span, span), span)
+
+    def sigmoid(v):
+        return 1.0 / (1.0 + jnp.exp(-v))
+
+    nt = (((1,), (1,)), ((), ()))
+    tn = (((0,), (0,)), ((), ()))
+    tile = 512 if width % 512 == 0 else width
+
+    def group(zp):
+        for j in range(PLANE):
+            tarrive(0, zp * PLANE + j)
+        x = tok[pl.ds(zp * PLANE, PLANE)].reshape(span, width)
+        g = lax.dot_general(wg[...], x, nt, preferred_element_type=F32)
+        u = lax.dot_general(wu[...], x, nt, preferred_element_type=F32)
+        gate_act[zp] = g
+        up_act[zp] = u
+        h = (g * sigmoid(g) * u).astype(BF16)
+        hid[:, lanes(zp)] = h
+        for n in range(width // tile):
+            cols = pl.ds(n * tile, tile)
+            v = lax.dot_general(h, wd[:, cols], tn, preferred_element_type=F32)
+            val[pl.ds(zp * PLANE, PLANE), :, cols] = v.astype(BF16).reshape(PLANE, pad, tile)
+        for j in range(PLANE):
+            vcopy(zp * PLANE + j).start()
+
+    def grad_group(zp):
+        for j in range(PLANE):
+            tarrive(1, zp * PLANE + j)
+        x = cot[pl.ds(zp * PLANE, PLANE)].reshape(span, width)
+        hg = lax.dot_general(wd[...], x, nt, preferred_element_type=F32)
+        g = gate_act[zp]
+        s = sigmoid(g)
+        ggrad[:, lanes(zp)] = (hg * up_act[zp] * s * (1.0 + g * (1.0 - s))).astype(BF16)
+        ugrad[:, lanes(zp)] = (hg * g * s).astype(BF16)
+
+    grads = ((ggrad, tok, wg, gg_hbm), (ugrad, tok, wu, gu_hbm), (hid, cot, wd, gd_hbm))
+    strip = 256 if width % 256 == 0 else width
+    strips = width // strip
+
+    def ocopy(g, n):
+        cols = pl.ds(pl.multiple_of(n * strip, strip), strip)
+        return pltpu.make_async_copy(
+            grads[g][2].at[:, cols], grads[g][3].at[0, :, cols], osem.at[g, n]
+        )
+
+    def grad_strip(n, carry):
+        cols = pl.ds(pl.multiple_of(n * strip, strip), strip)
+        for g, (left, right, out, _) in enumerate(grads):
+            r = right[:, :, cols].reshape(experts * pad, strip)
+            out[:, cols] = jnp.dot(left[...], r, preferred_element_type=F32).astype(BF16)
+            ocopy(g, n).start()
+        return carry
+
+    def bcopy(zp, r):
         return remote(
-            value_ref.at[b, :, other], partner_in.at[b], tsend.at[b], trecv.at[b], partner
-        )
-
-    def xcopy(zp, r):
-        return remote(
-            stage.at[zp, r], plane_in.at[zp, q], xsend.at[zp, r], xrecv.at[zp, q],
+            back.at[zp, r], plane_in.at[zp, q], bsend.at[zp, r], brecv.at[zp, q],
             (z * PLANE + mates[r], c),
         )
 
-    for i in range(line):
-        for r in (2, 0, 1, 3):
-            tcopy(order(i) * PLANE + (mates[r] if r < 3 else q)).start()
-    for i in range(line):
-        zp = order(i)
+    def give(zp):
         for r in (2, 0, 1, 3):
             b = zp * PLANE + (mates[r] if r < 3 else q)
-            tcopy(b).wait_recv()
-            total = (value_ref[b, :, mine].astype(F32) + partner_in[b].astype(F32)).astype(BF16)
+            vcopy(b).wait_recv()
+            total = (val[b, :, mine].astype(F32) + partner_in[b].astype(F32)).astype(BF16)
             if r < 3:
-                stage[zp, r] = total
-                xcopy(zp, r).start()
+                back[zp, r] = total
+                bcopy(zp, r).start()
             else:
                 plane_in[zp, q] = total
-
-    slot_id = lax.broadcasted_iota(jnp.int32, (pad, sel_rows), 0).astype(F32)
 
     def combine(zp):
         for r in range(3):
             remote(
-                stage.at[zp, r], plane_in.at[zp, mates[r]], xsend.at[zp, r],
-                xrecv.at[zp, mates[r]], partner,
+                back.at[zp, r], plane_in.at[zp, mates[r]], bsend.at[zp, r],
+                brecv.at[zp, mates[r]], partner,
             ).wait_recv()
         total = jnp.zeros((sel_rows, half), F32)
         for j in range(PLANE):
@@ -360,69 +384,126 @@
             both = jnp.concatenate([high, low], axis=0)
             values = plane_in[zp, j]
             total = total + lax.dot_general(
-                both, jnp.concatenate([values, values], axis=0),
-                (((0,), (0,)), ((), ())), preferred_element_type=F32,
+                both, jnp.concatenate([values, values], axis=0), tn, preferred_element_type=F32
             )
         acc[zp] = total
 
-    def zcopy(w, s):
+    def ucopy(w, s):
         to = d + (2 * w - 1) * PLANE
         return remote(
-            out_stage.at[w, s], line_in.at[w, s], zsend.at[w, s], zrecv.at[w, s], (to, c)
+            out_stage.at[w, s], line_in.at[w, s], usend.at[w, s], urecv.at[w, s], (to, c)
         )
 
     def height(w):
         return z if w == 1 else line - 1 - z
 
-    def sends(w, s):
+    def lifts(w, s):
         return (height(w) <= s) & (height(w) < line - 1)
 
-    def arrives(w, s):
+    def lands(w, s):
         return (height(w) > 0) & (height(w) - 1 <= s)
 
+    zstart(0, 0)
+    process(0, z)
+    reward_copy.wait()
+    scale[z] = sigmoid(part[0:1, :] + part_in[0:1, :]) * side_ref[z, experts : 2 * experts, :]
+    last = line - 2
+    for a in (0, 1):
+        for s in range(line - 1):
+            zwait(a, s)
+            if s < last:
+                zstart(a, s + 1)
+            elif a == 0:
+                loads[1].wait()
+                zstart(1, 0)
+            got(process, a, s)
+            if s == 0:
+                forward(a, z)
+            else:
+                got(forward, a, s - 1)
+            if a == 1:
+                if s == last:
+                    for i in range(line - 1):
+                        give(order(i))
+                    group(order(line - 1))
+                else:
+                    group(order(s + 1))
+        if a == 0:
+            process(1, z)
+        got(forward, a, last)
+        if a == 0:
+            for cp in loads[2:]:
+                cp.wait()
+            group(order(0))
+    give(z)
+
+    for i in range(line):
+        grad_group(order(line - 1 - i))
+    done = 0
     for s in range(line - 1):
         combine(order(s))
         if s > 0:
             for w in (1, 0):
-                @pl.when(arrives(w, s - 1))
+                @pl.when(lands(w, s - 1))
                 def _():
-                    zcopy(w, s - 1).wait_recv()
+                    ucopy(w, s - 1).wait_recv()
         for w in (1, 0):
             blk = z + (2 * w - 1) * (line - 1 - s)
 
-            @pl.when(sends(w, s) & (height(w) > 0))
+            @pl.when(lifts(w, s) & (height(w) > 0))
             def _():
                 if s > 0:
                     out_stage[w, s] = (acc[blk] + line_in[w, s - 1].astype(F32)).astype(BF16)
-                    zcopy(w, s).start()
-
-            @pl.when(sends(w, s) & (height(w) == 0))
+                    ucopy(w, s).start()
+
+            @pl.when(lifts(w, s) & (height(w) == 0))
             def _():
                 out_stage[w, s] = acc[blk].astype(BF16)
-                zcopy(w, s).start()
+                ucopy(w, s).start()
+        upto = strips * (s + 1) // line
+        lax.fori_loop(done, upto, grad_strip, 0)
+        done = upto
     combine(z)
-    final = line - 2
+    lax.fori_loop(done, strips, grad_strip, 0)
     for w in (1, 0):
-        @pl.when(arrives(w, final))
+        @pl.when(lands(w, last))
         def _():
-            zcopy(w, final).wait_recv()
-            acc[z] = acc[z] + line_in[w, final].astype(F32)
+            ucopy(w, last).wait_recv()
+            acc[z] = acc[z] + line_in[w, last].astype(F32)
     mixed_ref[...] = acc[z].astype(BF16)
 
+    for g in range(3):
+        for n in range(strips):
+            ocopy(g, n).wait()
     for b in range(experts):
-        tcopy(b).wait_send()
+        vcopy(b).wait_send()
+        for a in (0, 1):
+            tcopy(a, b).wait_send()
     for zp in range(line):
         for r in range(3):
-            xcopy(zp, r).wait_send()
+            bcopy(zp, r).wait_send()
+            for a in (0, 1):
+                xcopy(a, zp, r).wait_send()
     for s in range(line - 1):
         for w in (1, 0):
-            @pl.when(sends(w, s))
+            @pl.when(lifts(w, s))
             def _():
-                zcopy(w, s).wait_send()
+                ucopy(w, s).wait_send()
+
+        for a in (0, 1):
+            for way in (1, -1):
+                @pl.when(sends(a, s, way))
+                def _():
+                    for cp in zcopies(a, s, way):
+                        cp.wait_send()
 
 
 def vmem(count):
     return [pl.BlockSpec(memory_space=pltpu.VMEM)] * count
+
+
+def hbm(count):
+    return [pl.BlockSpec(memory_space=pl.ANY)] * count
 
 
 DMA = pltpu.SemaphoreType.DMA
@@ -436,68 +517,46 @@
     capacity = 5 * sel_rows * top // (4 * experts)
     pad = -(-capacity // 16) * 16
     half = target.shape[1]
-    width = w_gate.shape[2]
-    sel = (select - lax.axis_index("dp") * pool.shape[0]).reshape(sel_rows, 1)
-    rw = jnp.broadcast_to(reward_w[None, :], (16, half))
-    rows_shape = jax.ShapeDtypeStruct((experts, pad, width), BF16)
-    tokens, cots, side = pl.pallas_call(
-        functools.partial(dispatch_kernel, line, pad),
-        name="dispatch",
-        out_shape=(
-            rows_shape, rows_shape, jax.ShapeDtypeStruct((line, 2 * experts, sel_rows), F32)
-        ),
-        in_specs=vmem(6),
-        out_specs=tuple(vmem(3)),
+    units, width = w_gate.shape[1:]
+    span = PLANE * pad
+    grad_shape = jax.ShapeDtypeStruct(w_gate.shape, BF16)
+    mat = pltpu.VMEM((units, width), BF16)
+    slots = pltpu.VMEM((experts, pad, width), BF16)
+    act = pltpu.VMEM((line, units, span), F32)
+    flat = pltpu.VMEM((units, experts * pad), BF16)
+    return pl.pallas_call(
+        functools.partial(layer_kernel, line, pad),
+        name="layer",
+        out_shape=(jax.ShapeDtypeStruct((sel_rows, half), BF16), grad_shape, grad_shape, grad_shape),
+        in_specs=hbm(1) + vmem(4) + hbm(4),
+        out_specs=tuple(vmem(1) + hbm(3)),
         scratch_shapes=[
+            pltpu.VMEM(pool.shape, BF16), pltpu.VMEM((2, sel_rows, sel_rows), F32),
+            mat, mat, mat, slots, slots, act, act, flat, flat, flat, slots,
             pltpu.VMEM((2, line, sel_rows, half), BF16),
+            pltpu.VMEM((line, 2 * experts, sel_rows), F32),
             pltpu.VMEM((line, experts, sel_rows), F32),
             pltpu.VMEM((16, sel_rows), F32),
             pltpu.VMEM((16, sel_rows), F32),
             pltpu.VMEM((2, line, 3, pad, half), BF16),
-            DMA((2, 2, line)), DMA((2, line)), DMA((2, line)), DMA((line,)),
-            DMA((2, line)), DMA((line,)), DMA((2, line, 3)), DMA((2, experts)),
-            DMA((2, experts)), DMA((2, experts)), DMA, DMA,
-        ],
-        compiler_params=pltpu.CompilerParams(
-            collective_id=0, has_side_effects=True, vmem_limit_bytes=50 * 2**20
-        ),
-    )(pool, sel, rw, routes.T, gates.T, target)
-    token_rows = tokens.reshape(experts * pad, width)
-    cot_rows = cots.reshape(experts * pad, width)
-    wg, wu, wd = w_gate[0], w_up[0], w_down[0]
-    dot = functools.partial(jnp.einsum, preferred_element_type=F32)
-    gate_act = dot("rd,fd->rf", token_rows, wg)
-    up_act = dot("rd,fd->rf", token_rows, wu)
-    sig = jax.nn.sigmoid(gate_act)
-    hidden = (gate_act * sig * up_act).astype(BF16)
-    value = dot("rf,fd->rd", hidden, wd).astype(BF16).reshape(experts, pad, width)
-    mixed = pl.pallas_call(
-        functools.partial(return_kernel, line, pad),
-        name="give_back",
-        out_shape=jax.ShapeDtypeStruct((sel_rows, half), BF16),
-        in_specs=vmem(2),
-        out_specs=vmem(1)[0],
-        scratch_shapes=[
             pltpu.VMEM((experts, pad, half), BF16),
             pltpu.VMEM((line, 3, pad, half), BF16),
             pltpu.VMEM((line, PLANE, pad, half), BF16),
             pltpu.VMEM((line, sel_rows, half), F32),
-            pltpu.VMEM((2, line, sel_rows, half), BF16),
-            pltpu.VMEM((2, line, sel_rows, half), BF16),
+            pltpu.VMEM((2, line - 1, sel_rows, half), BF16),
+            pltpu.VMEM((2, line - 1, sel_rows, half), BF16),
+            DMA((5,)), DMA((3, width // 256)),
+            DMA((2, 2, line)), DMA((2, line)), DMA((2, line)), DMA((line,)),
+            DMA((2, line)), DMA((line,)), DMA((2, line, 3)), DMA((2, experts)),
+            DMA((2, experts)), DMA((2, experts)), DMA, DMA,
             DMA((experts,)), DMA((experts,)), DMA((line, 3)), DMA((line, PLANE)),
             DMA((2, line)), DMA((2, line)),
         ],
         compiler_params=pltpu.CompilerParams(
-            collective_id=1, has_side_effects=True, vmem_limit_bytes=50 * 2**20
+            collective_id=0, has_side_effects=True, vmem_limit_bytes=67043328
         ),
-    )(value, side)
-    hidden_grad = dot("rd,fd->rf", cot_rows, wd)
-    gate_grad = (hidden_grad * up_act * sig * (1.0 + gate_act * (1.0 - sig))).astype(BF16)
-    up_grad = (hidden_grad * gate_act * sig).astype(BF16)
-    grad_down = dot("rf,rd->fd", hidden, cot_rows).astype(BF16)[None]
-    grad_gate = dot("rf,rd->fd", gate_grad, token_rows).astype(BF16)[None]
-    grad_up = dot("rf,rd->fd", up_grad, token_rows).astype(BF16)[None]
-    return mixed, grad_gate, grad_up, grad_down
+    )(pool, select.reshape(1, sel_rows), reward_w.reshape(1, half), routes, gates, target,
+      w_gate, w_up, w_down)
 
 
 def solution(mesh):

time: 134 us -> 107 us (0.80)
  matrix products: 31.9 us -> 0 us
  local copies, waits for them, and re-layouts: 4.89 us -> 14.1 us
  Pallas kernels: 95 us -> 91.2 us
    dot_general x7 -> x0, matrix products: 31.9 us -> none  [the longest x1 6.01 us: planar(): gate_act = dot('rd,fd->rf', token_rows, wg)]
    unnamed x17 -> x10, local copies, waits for them, and re-layouts: 4.09 us -> 12.9 us
    pallas_call x2 -> x1, Pallas kernels: 95 us -> 91.2 us  [planar(): pl.pallas_call(functools.partial(layer_kernel, line, pad), name='layer',...]
where the time goes in v2:
time: 107 us; the launch traced here: 106 us
  Pallas kernels  91.2 us (85%)
  local copies, waits for them, and re-layouts  14.1 us (13%)
    pallas_call x1, Pallas kernels, planar(): pl.pallas_call(functools.partial(layer_kernel, line, pad), name='layer',...  91.2 us
    unnamed x10, local copies, waits for them, and re-layouts  12.9 us

profile of v2, /device:TPU:0, one launch (start us, length us, event | category | flops | bytes accessed | tf_op | source)
XLA Modules:
  0.0 105.9 jit_solution(10726431946653468844)
XLA Ops:
  0.6 1.3 %reshape.15.rw_ref = bf16[1,1024]{1,0:T(2,128)(2,1)} reshape(bf16[1024]{0:T(1024)(128)(2,1)} %param.11) | data formatting | bytes 4096 | tf_op jit(solution)/shard_map/reshape | solution.py:558
  1.9 1.4 %copy.13.rt_ref = s32[128,6]{1,0:T(8,128)} copy(s32[128,6]{0,1:T(8,128)} %param.12) | data formatting | bytes 6144 | tf_op args[3]
  3.3 1.4 %copy.14.gt_ref = f32[128,6]{1,0:T(8,128)} copy(f32[128,6]{0,1:T(8,128)} %param.13) | data formatting | bytes 6144 | tf_op args[4]
  4.8 91.2 %layer.1 = (bf16[128,1024]{1,0:T(8,128)(2,1)}, bf16[1,704,2048]{2,1,0:T(8,128)(2,1)}, bf16[1,704,2048]{2,1,0:T(8,128)(2,1)}, bf16[1,704,2048]{2,1,0:T(8,128)(2,1)}) custom-call(bf16[256,1024]{1,0:T(8,128)(2,1)} %pool_hbm.1, s32[1,128]{1,0:T(1,128)} %bitcast.1, bf16[1,1024]{1,0:T(2,128)(2,1)} %reshape.15.rw_ref, s32[128,6]{1,0:T(8,128)} %copy.13.rt_ref, ...), custom_call_target="tpu_custom_call" | custom-call | tf_op jit(solution)/shard_map/layer/pallas_call | solution.py:527
  95.9 1.7 %copy.19 = bf16[128,1024]{1,0:T(8,128)(2,1)} copy(bf16[128,1024]{1,0:T(8,128)(2,1)} %get-tuple-element.8) | data formatting | bytes 524288
  97.6 0.0 copy-start.1
  97.6 3.9 %copy.20 = bf16[1,704,2048]{2,1,0:T(8,128)(2,1)} copy(bf16[1,704,2048]{2,1,0:T(8,128)(2,1)} %get-tuple-element.9) | data formatting | bytes 5767168
  101.5 0.0 copy-done.1
  101.5 0.0 copy-start
  101.5 1.6 %copy.21 = bf16[1,704,2048]{2,1,0:T(8,128)(2,1)} copy(bf16[1,704,2048]{2,1,0:T(8,128)(2,1)S(1)} %copy-done.1) | data formatting | bytes 5767168
  103.1 1.3 %copy-done = bf16[1,704,2048]{2,1,0:T(8,128)(2,1)S(1)} copy-done((bf16[1,704,2048]{2,1,0:T(8,128)(2,1)S(1)}, bf16[1,704,2048]{2,1,0:T(8,128)(2,1)}, u32[]{:S(2)}) %copy-start) | copy-done | bytes 2883608
  104.4 1.6 %copy.22 = bf16[1,704,2048]{2,1,0:T(8,128)(2,1)} copy(bf16[1,704,2048]{2,1,0:T(8,128)(2,1)S(1)} %copy-done) | data formatting | bytes 5767168
Async XLA Ops:
  97.6 3.9 %copy-start.1 = (bf16[1,704,2048]{2,1,0:T(8,128)(2,1)S(1)}, bf16[1,704,2048]{2,1,0:T(8,128)(2,1)}, u32[]{:S(2)}) copy-start(bf16[1,704,2048]{2,1,0:T(8,128)(2,1)} %get-tuple-element.10) | copy-start | bytes 8650756
  101.5 2.9 %copy-start = (bf16[1,704,2048]{2,1,0:T(8,128)(2,1)S(1)}, bf16[1,704,2048]{2,1,0:T(8,128)(2,1)}, u32[]{:S(2)}) copy-start(bf16[1,704,2048]{2,1,0:T(8,128)(2,1)} %get-tuple-element.11) | copy-start | bytes 8650756

commit v3 on v2

--- a/solution.py
+++ b/solution.py
@@ -100,16 +100,14 @@
         pl.semaphore_signal(barrier, inc=1, device_id=(z * PLANE + m, c), device_id_type=MESH)
     pl.semaphore_signal(barrier, inc=1, device_id=(d, 1 - c), device_id_type=MESH)
 
-    @pl.when(z > 0)
-    def _():
-        pl.semaphore_signal(barrier, inc=1, device_id=(d - PLANE, c), device_id_type=MESH)
-
-    @pl.when(z < line - 1)
-    def _():
-        pl.semaphore_signal(barrier, inc=1, device_id=(d + PLANE, c), device_id_type=MESH)
-
-    below, above = (z + line - 1) // line, (2 * line - 2 - z) // line
-    pl.semaphore_wait(barrier, 4 + below + above)
+    for k in range(1, line):
+        pl.semaphore_signal(
+            barrier, inc=1, device_id=((z + k) % line * PLANE + q, c), device_id_type=MESH
+        )
+
+
+def greeted(line):
+    pl.semaphore_wait(pltpu.get_barrier_semaphore(), PLANE + line - 1)
 
 
 def remote(src, dst, send, recv, dev):
@@ -120,17 +118,18 @@
 
 def layer_kernel(
     line, pad, pool_hbm, sel_ref, rw_ref, rt_ref, gt_ref, target_hbm, wg_hbm, wu_hbm, wd_hbm,
-    mixed_ref, gg_hbm, gu_hbm, gd_hbm,
-    pool_ref, wide, wg, wu, wd, tok, cot, gate_act, up_act, hid, ggrad, ugrad, val,
+    mixed_ref, gg_ref, gu_ref, gd_ref,
+    pool_ref, rt_vmem, gt_vmem, tok, cot, gate_act, up_act, hid, ggrad, ugrad, val,
     data, side_ref, scale, part, part_in, stage,
     partner_in, back, plane_in, acc, out_stage, line_in,
-    lsem, osem, zsend, zrecv, ssend, srecv, csend, crecv, xsend, xrecv, tsend, trecv, psend, precv,
+    lsem, zsend, zrecv, ssend, srecv, csend, crecv, xsend, xrecv, tsend, trecv, psend, precv,
     vsend, vrecv, bsend, brecv, usend, urecv,
 ):
     d, c, z, q, mates = place(line)
     experts = line * PLANE
     sel_rows, half = mixed_ref.shape
-    top = gt_ref.shape[1]
+    top = gt_ref.shape[0]
+    wg, wu, wd = gg_ref.at[0], gu_ref.at[0], gd_ref.at[0]
     units, width = wg.shape
     span = PLANE * pad
     rows = (tok, cot)
@@ -142,27 +141,26 @@
     def order(i):
         return (z + turn * (1 + i) + 2 * line) % line
 
+    greet(d, c, z, q, mates, line)
     loads = [
         pltpu.make_async_copy(src, dst, lsem.at[i])
         for i, (src, dst) in enumerate((
             (pool_hbm, pool_ref), (target_hbm, data.at[1, z]), (wg_hbm.at[0], wg),
-            (wu_hbm.at[0], wu), (wd_hbm.at[0], wd),
+            (wu_hbm.at[0], wu), (wd_hbm.at[0], wd), (rt_ref, rt_vmem), (gt_ref, gt_vmem),
         ))
     ]
-    for cp in loads:
-        cp.start()
-
-    wide[0, :, 0:top] = rt_ref[...].astype(F32)
-    wide[1, :, 0:top] = gt_ref[...]
-    routes_t = wide[0].T
-    gates_t = wide[1].T
-    expert_id = lax.broadcasted_iota(jnp.int32, (experts, sel_rows), 0).astype(F32)
+    for i in (5, 6, 0, 1, 2, 3, 4):
+        loads[i].start()
+
+    loads[5].wait()
+    loads[6].wait()
+    expert_id = lax.broadcasted_iota(jnp.int32, (experts, sel_rows), 0)
     member = jnp.zeros((experts, sel_rows), F32)
     gate = jnp.zeros((experts, sel_rows), F32)
     for k in range(top):
-        eq = routes_t[k : k + 1, :] == expert_id
+        eq = rt_vmem[k : k + 1, :] == expert_id
         member = member + jnp.where(eq, 1.0, 0.0)
-        gate = gate + jnp.where(eq, gates_t[k : k + 1, :], 0.0)
+        gate = gate + jnp.where(eq, gt_vmem[k : k + 1, :], 0.0)
     tri = jnp.where(
         lax.broadcasted_iota(jnp.int32, (sel_rows, sel_rows), 0)
         < lax.broadcasted_iota(jnp.int32, (sel_rows, sel_rows), 1),
@@ -183,11 +181,11 @@
     ).astype(BF16)
     data[0, z] = chosen
     part[...] = lax.dot_general(
-        jnp.broadcast_to(rw_ref[...].astype(F32), (16, half)).astype(BF16), chosen,
+        rw_ref[...], chosen,
         (((1,), (1,)), ((), ())), preferred_element_type=F32,
     )
 
-    greet(d, c, z, q, mates, line)
+    greeted(line)
     reward_copy = remote(part, part_in, psend, precv, partner)
     reward_copy.start()
 
@@ -195,18 +193,34 @@
         blk = z - way * s
         dev = (d + way * PLANE, c)
         w = (way + 1) // 2
-        main = remote(data.at[a, blk], data.at[a, blk], zsend.at[a, w, s], zrecv.at[a, blk], dev)
-        if a == 0:
-            extra = remote(
-                side_ref.at[blk], side_ref.at[blk], ssend.at[w, s], srecv.at[blk], dev
-            )
-        else:
-            extra = remote(scale.at[blk], scale.at[blk], csend.at[w, s], crecv.at[blk], dev)
-        return extra, main
+        return (
+            remote(side_ref.at[blk], side_ref.at[blk], ssend.at[w, s], srecv.at[blk], dev),
+            remote(data.at[0, blk], data.at[0, blk], zsend.at[0, w, s], zrecv.at[0, blk], dev),
+        )
 
     def sends(a, s, way):
         blk, to = z - way * s, z + way
         return (blk >= 0) & (blk < line) & (to >= 0) & (to < line)
+
+    def lcopy(k, way):
+        w = (way + 1) // 2
+        dev = (d + way * k * PLANE, c)
+        return (
+            remote(scale.at[z], scale.at[z], csend.at[w, k], crecv.at[z], dev),
+            remote(data.at[1, z], data.at[1, z], zsend.at[1, w, k], zrecv.at[1, z], dev),
+        )
+
+    def reaches(k, way):
+        to = z + way * k
+        return (to >= 0) & (to < line)
+
+    def lstart():
+        for k in range(1, line):
+            for way in (1, -1):
+                @pl.when(reaches(k, way))
+                def _():
+                    for cp in lcopy(k, way):
+                        cp.start()
 
     def zstart(a, s):
         for way in (1, -1):
@@ -330,22 +344,15 @@
         ggrad[:, lanes(zp)] = (hg * up_act[zp] * s * (1.0 + g * (1.0 - s))).astype(BF16)
         ugrad[:, lanes(zp)] = (hg * g * s).astype(BF16)
 
-    grads = ((ggrad, tok, wg, gg_hbm), (ugrad, tok, wu, gu_hbm), (hid, cot, wd, gd_hbm))
+    grads = ((ggrad, tok, wg), (ugrad, tok, wu), (hid, cot, wd))
     strip = 256 if width % 256 == 0 else width
     strips = width // strip
 
-    def ocopy(g, n):
-        cols = pl.ds(pl.multiple_of(n * strip, strip), strip)
-        return pltpu.make_async_copy(
-            grads[g][2].at[:, cols], grads[g][3].at[0, :, cols], osem.at[g, n]
-        )
-
     def grad_strip(n, carry):
         cols = pl.ds(pl.multiple_of(n * strip, strip), strip)
-        for g, (left, right, out, _) in enumerate(grads):
+        for left, right, out in grads:
             r = right[:, :, cols].reshape(experts * pad, strip)
             out[:, cols] = jnp.dot(left[...], r, preferred_element_type=F32).astype(BF16)
-            ocopy(g, n).start()
         return carry
 
     def bcopy(zp, r):
@@ -411,11 +418,11 @@
     for a in (0, 1):
         for s in range(line - 1):
             zwait(a, s)
-            if s < last:
+            if a == 0 and s < last:
                 zstart(a, s + 1)
             elif a == 0:
                 loads[1].wait()
-                zstart(1, 0)
+                lstart()
             got(process, a, s)
             if s == 0:
                 forward(a, z)
@@ -432,7 +439,7 @@
             process(1, z)
         got(forward, a, last)
         if a == 0:
-            for cp in loads[2:]:
+            for cp in loads[2:5]:
                 cp.wait()
             group(order(0))
     give(z)
@@ -472,9 +479,6 @@
             acc[z] = acc[z] + line_in[w, last].astype(F32)
     mixed_ref[...] = acc[z].astype(BF16)
 
-    for g in range(3):
-        for n in range(strips):
-            ocopy(g, n).wait()
     for b in range(experts):
         vcopy(b).wait_send()
         for a in (0, 1):
@@ -490,12 +494,16 @@
             def _():
                 ucopy(w, s).wait_send()
 
-        for a in (0, 1):
-            for way in (1, -1):
-                @pl.when(sends(a, s, way))
-                def _():
-                    for cp in zcopies(a, s, way):
-                        cp.wait_send()
+        for way in (1, -1):
+            @pl.when(sends(0, s, way))
+            def _():
+                for cp in zcopies(0, s, way):
+                    cp.wait_send()
+
+            @pl.when(reaches(s + 1, way))
+            def _():
+                for cp in lcopy(s + 1, way):
+                    cp.wait_send()
 
 
 def vmem(count):
@@ -519,20 +527,20 @@
     half = target.shape[1]
     units, width = w_gate.shape[1:]
     span = PLANE * pad
-    grad_shape = jax.ShapeDtypeStruct(w_gate.shape, BF16)
-    mat = pltpu.VMEM((units, width), BF16)
+    grad_shape = pltpu.VMEM(w_gate.shape, BF16)
+    rw = jnp.broadcast_to(reward_w[None, :], (16, half))
     slots = pltpu.VMEM((experts, pad, width), BF16)
     act = pltpu.VMEM((line, units, span), F32)
     flat = pltpu.VMEM((units, experts * pad), BF16)
     return pl.pallas_call(
         functools.partial(layer_kernel, line, pad),
         name="layer",
-        out_shape=(jax.ShapeDtypeStruct((sel_rows, half), BF16), grad_shape, grad_shape, grad_shape),
-        in_specs=hbm(1) + vmem(4) + hbm(4),
-        out_specs=tuple(vmem(1) + hbm(3)),
+        out_shape=(pltpu.VMEM((sel_rows, half), BF16), grad_shape, grad_shape, grad_shape),
+        in_specs=hbm(1) + vmem(2) + hbm(6),
+        out_specs=tuple(vmem(4)),
         scratch_shapes=[
-            pltpu.VMEM(pool.shape, BF16), pltpu.VMEM((2, sel_rows, sel_rows), F32),
-            mat, mat, mat, slots, slots, act, act, flat, flat, flat, slots,
+            pltpu.VMEM(pool.shape, BF16), pltpu.VMEM((top, sel_rows), jnp.int32),
+            pltpu.VMEM((top, sel_rows), F32), slots, slots, act, act, flat, flat, flat, slots,
             pltpu.VMEM((2, line, sel_rows, half), BF16),
             pltpu.VMEM((line, 2 * experts, sel_rows), F32),
             pltpu.VMEM((line, experts, sel_rows), F32),
@@ -545,7 +553,7 @@
             pltpu.VMEM((line, sel_rows, half), F32),
             pltpu.VMEM((2, line - 1, sel_rows, half), BF16),
             pltpu.VMEM((2, line - 1, sel_rows, half), BF16),
-            DMA((5,)), DMA((3, width // 256)),
+            DMA((7,)),
             DMA((2, 2, line)), DMA((2, line)), DMA((2, line)), DMA((line,)),
             DMA((2, line)), DMA((line,)), DMA((2, line, 3)), DMA((2, experts)),
             DMA((2, experts)), DMA((2, experts)), DMA, DMA,
@@ -553,9 +561,9 @@
             DMA((2, line)), DMA((2, line)),
         ],
         compiler_params=pltpu.CompilerParams(
-            collective_id=0, has_side_effects=True, vmem_limit_bytes=67043328
+            collective_id=0, has_side_effects=True, vmem_limit_bytes=57 * 10**6
         ),
-    )(pool, select.reshape(1, sel_rows), reward_w.reshape(1, half), routes, gates, target,
+    )(pool, select.reshape(1, sel_rows), rw, routes.T, gates.T, target,
       w_gate, w_up, w_down)
 
 

time: 107 us -> 106 us (level)
  local copies, waits for them, and re-layouts: 14.1 us -> 6.74 us
  Pallas kernels: 91.2 us -> 97.2 us
    unnamed x10 -> x4, local copies, waits for them, and re-layouts: 12.9 us -> 5.44 us
    pallas_call x1, Pallas kernels: 91.2 us -> 97.2 us  [planar(): pl.pallas_call(functools.partial(layer_kernel, line, pad), name='layer',...]
    broadcast_in_dim x0 -> x1, local copies, waits for them, and re-layouts: none -> 1.3 us  [planar(): rw = jnp.broadcast_to(reward_w[None, :], (16, half))]
    reshape x1 -> x0, local copies, waits for them, and re-layouts: 1.28 us -> none  [planar(): reward_w.reshape(1, half)]
where the time goes in v3:
time: 106 us; the launch traced here: 105 us
  Pallas kernels  97.2 us (92%)
  local copies, waits for them, and re-layouts  6.74 us (6%)
    pallas_call x1, Pallas kernels, planar(): pl.pallas_call(functools.partial(layer_kernel, line, pad), name='layer',...  97.2 us
    unnamed x4, local copies, waits for them, and re-layouts  5.44 us

profile of v3, /device:TPU:0, one launch (start us, length us, event | category | flops | bytes accessed | tf_op | source)
XLA Modules:
  0.0 104.6 jit_solution(18274143547239543620)
XLA Ops:
  0.6 1.3 %broadcast_in_dim.2.rw_ref = bf16[16,1024]{1,0:T(8,128)(2,1)} broadcast(bf16[1024]{0:T(1024)(128)(2,1)} %param.11), dimensions={1} | broadcast | bytes 34816 | tf_op jit(solution)/shard_map/broadcast_in_dim | solution.py:531
  1.9 97.2 %layer.1 = (bf16[128,1024]{1,0:T(8,128)(2,1)S(1)}, bf16[1,704,2048]{2,1,0:T(8,128)(2,1)S(1)}, bf16[1,704,2048]{2,1,0:T(8,128)(2,1)S(1)}, bf16[1,704,2048]{2,1,0:T(8,128)(2,1)S(1)}) custom-call(bf16[256,1024]{1,0:T(8,128)(2,1)} %pool_hbm.1, s32[1,128]{1,0:T(1,128)} %bitcast.5, bf16[16,1024]{1,0:T(8,128)(2,1)} %broadcast_in_dim.2.rw_ref, s32[6,128]{1,0:T(8,128)} %bitcast.3, ...), custom_call_target="tpu_custom_call" | custom-call | tf_op jit(solution)/shard_map/layer/pallas_call | solution.py:535
  99.1 0.7 copy.17
  99.8 1.6 %copy.18 = bf16[1,704,2048]{2,1,0:T(8,128)(2,1)} copy(bf16[1,704,2048]{2,1,0:T(8,128)(2,1)S(1)} %get-tuple-element.5) | data formatting | bytes 5767168
  101.4 1.6 %copy.19 = bf16[1,704,2048]{2,1,0:T(8,128)(2,1)} copy(bf16[1,704,2048]{2,1,0:T(8,128)(2,1)S(1)} %get-tuple-element.6) | data formatting | bytes 5767168
  103.0 1.6 %copy.20 = bf16[1,704,2048]{2,1,0:T(8,128)(2,1)} copy(bf16[1,704,2048]{2,1,0:T(8,128)(2,1)S(1)} %get-tuple-element.7) | data formatting | bytes 5767168

commit v4 on v3

--- a/solution.py
+++ b/solution.py
@@ -100,14 +100,18 @@
         pl.semaphore_signal(barrier, inc=1, device_id=(z * PLANE + m, c), device_id_type=MESH)
     pl.semaphore_signal(barrier, inc=1, device_id=(d, 1 - c), device_id_type=MESH)
 
-    for k in range(1, line):
-        pl.semaphore_signal(
-            barrier, inc=1, device_id=((z + k) % line * PLANE + q, c), device_id_type=MESH
-        )
-
-
-def greeted(line):
-    pl.semaphore_wait(pltpu.get_barrier_semaphore(), PLANE + line - 1)
+    @pl.when(z > 0)
+    def _():
+        pl.semaphore_signal(barrier, inc=1, device_id=(d - PLANE, c), device_id_type=MESH)
+
+    @pl.when(z < line - 1)
+    def _():
+        pl.semaphore_signal(barrier, inc=1, device_id=(d + PLANE, c), device_id_type=MESH)
+
+
+def greeted(z, line):
+    below, above = (z + line - 1) // line, (2 * line - 2 - z) // line
+    pl.semaphore_wait(pltpu.get_barrier_semaphore(), 4 + below + above)
 
 
 def remote(src, dst, send, recv, dev):
@@ -185,7 +189,7 @@
         (((1,), (1,)), ((), ())), preferred_element_type=F32,
     )
 
-    greeted(line)
+    greeted(z, line)
     reward_copy = remote(part, part_in, psend, precv, partner)
     reward_copy.start()
 
@@ -193,34 +197,18 @@
         blk = z - way * s
         dev = (d + way * PLANE, c)
         w = (way + 1) // 2
-        return (
-            remote(side_ref.at[blk], side_ref.at[blk], ssend.at[w, s], srecv.at[blk], dev),
-            remote(data.at[0, blk], data.at[0, blk], zsend.at[0, w, s], zrecv.at[0, blk], dev),
-        )
+        main = remote(data.at[a, blk], data.at[a, blk], zsend.at[a, w, s], zrecv.at[a, blk], dev)
+        if a == 0:
+            extra = remote(
+                side_ref.at[blk], side_ref.at[blk], ssend.at[w, s], srecv.at[blk], dev
+            )
+        else:
+            extra = remote(scale.at[blk], scale.at[blk], csend.at[w, s], crecv.at[blk], dev)
+        return extra, main
 
     def sends(a, s, way):
         blk, to = z - way * s, z + way
         return (blk >= 0) & (blk < line) & (to >= 0) & (to < line)
-
-    def lcopy(k, way):
-        w = (way + 1) // 2
-        dev = (d + way * k * PLANE, c)
-        return (
-            remote(scale.at[z], scale.at[z], csend.at[w, k], crecv.at[z], dev),
-            remote(data.at[1, z], data.at[1, z], zsend.at[1, w, k], zrecv.at[1, z], dev),
-        )
-
-    def reaches(k, way):
-        to = z + way * k
-        return (to >= 0) & (to < line)
-
-    def lstart():
-        for k in range(1, line):
-            for way in (1, -1):
-                @pl.when(reaches(k, way))
-                def _():
-                    for cp in lcopy(k, way):
-                        cp.start()
 
     def zstart(a, s):
         for way in (1, -1):
@@ -418,11 +406,11 @@
     for a in (0, 1):
         for s in range(line - 1):
             zwait(a, s)
-            if a == 0 and s < last:
+            if s < last:
                 zstart(a, s + 1)
             elif a == 0:
                 loads[1].wait()
-                lstart()
+                zstart(1, 0)
             got(process, a, s)
             if s == 0:
                 forward(a, z)
@@ -494,16 +482,12 @@
             def _():
                 ucopy(w, s).wait_send()
 
-        for way in (1, -1):
-            @pl.when(sends(0, s, way))
-            def _():
-                for cp in zcopies(0, s, way):
-                    cp.wait_send()
-
-            @pl.when(reaches(s + 1, way))
-            def _():
-                for cp in lcopy(s + 1, way):
-                    cp.wait_send()
+        for a in (0, 1):
+            for way in (1, -1):
+                @pl.when(sends(a, s, way))
+                def _():
+                    for cp in zcopies(a, s, way):
+                        cp.wait_send()
 
 
 def vmem(count):

time: 106 us -> 100 us (0.943); the launches traced: 105 us -> 100 us
  Pallas kernels: 97.2 us -> 92.8 us
    pallas_call x1, Pallas kernels: 97.2 us -> 92.8 us  [planar(): pl.pallas_call(functools.partial(layer_kernel, line, pad), name='layer',...]
where the time goes in v4:
time: 100 us
  Pallas kernels  92.8 us (93%)
  local copies, waits for them, and re-layouts  6.74 us (7%)
    pallas_call x1, Pallas kernels, planar(): pl.pallas_call(functools.partial(layer_kernel, line, pad), name='layer',...  92.8 us
    unnamed x4, local copies, waits for them, and re-layouts  5.44 us

profile of v4, /device:TPU:0, one launch (start us, length us, event | category | flops | bytes accessed | tf_op | source)
XLA Modules:
  0.0 100.2 jit_solution(1681344042717485046)
XLA Ops:
  0.6 1.3 %broadcast_in_dim.2.rw_ref = bf16[16,1024]{1,0:T(8,128)(2,1)} broadcast(bf16[1024]{0:T(1024)(128)(2,1)} %param.11), dimensions={1} | broadcast | bytes 34816 | tf_op jit(solution)/shard_map/broadcast_in_dim | solution.py:515
  1.9 92.8 %layer.1 = (bf16[128,1024]{1,0:T(8,128)(2,1)S(1)}, bf16[1,704,2048]{2,1,0:T(8,128)(2,1)S(1)}, bf16[1,704,2048]{2,1,0:T(8,128)(2,1)S(1)}, bf16[1,704,2048]{2,1,0:T(8,128)(2,1)S(1)}) custom-call(bf16[256,1024]{1,0:T(8,128)(2,1)} %pool_hbm.1, s32[1,128]{1,0:T(1,128)} %bitcast.5, bf16[16,1024]{1,0:T(8,128)(2,1)} %broadcast_in_dim.2.rw_ref, s32[6,128]{1,0:T(8,128)} %bitcast.3, ...), custom_call_target="tpu_custom_call" | custom-call | tf_op jit(solution)/shard_map/layer/pallas_call | solution.py:519
  94.8 0.7 copy.17
  95.5 1.6 %copy.18 = bf16[1,704,2048]{2,1,0:T(8,128)(2,1)} copy(bf16[1,704,2048]{2,1,0:T(8,128)(2,1)S(1)} %get-tuple-element.5) | data formatting | bytes 5767168
  97.0 1.6 %copy.19 = bf16[1,704,2048]{2,1,0:T(8,128)(2,1)} copy(bf16[1,704,2048]{2,1,0:T(8,128)(2,1)S(1)} %get-tuple-element.6) | data formatting | bytes 5767168
  98.6 1.6 %copy.20 = bf16[1,704,2048]{2,1,0:T(8,128)(2,1)} copy(bf16[1,704,2048]{2,1,0:T(8,128)(2,1)S(1)} %get-tuple-element.7) | data formatting | bytes 5767168
